TPU v7x, 32 devices: a whole 2x2x4 slice. The times are simulated.
32 devices in a mesh: row: 4 (over x, core), col: 8 (over z, y).
Axes of the slice: x: 2, y: 2, z: 4, core: 2. Of those that a mesh axis runs over, the one named last changes fastest.
Arguments:
- amplitudes: bfloat16 [16384, 4096], P(('row', 'col')), may hold values from -6 to 6
- live_tiles: int32 [256, 32], P(('row', 'col')), may hold values 0 or 1
- destination: int32 [256], P(('row', 'col')), may hold values from 0 to 255, as said below
- integral_list: int32 [32, 2], replicated, may hold values from 0 to 31, as said below
- integral_tiles: bfloat16 [32, 128, 128], P(('row', 'col')), may hold values from -0.25 to 0.25
Outputs:
- ladder: bfloat16 [16384, 1024], P(('row', 'col'))
Inputs may be any that keep to these rules, and one draw needn't show every extreme that they name: destination is a permutation of the pair tiles that keeps each tile within its row group (8 consecutive devices in row+col order); of one device's 8 stored tiles at most 2 have their output on any one device, and some device reaches 2 in every draw. `integral_list`: the (c, d) tile comes first and is below 32, the (a, b) tile second and below 8; no pair of tiles is listed twice.
All inputs are finite; a program needn't handle non-finite values. No bound on the sum of `live_tiles` on one device may be relied on, other than what follows from the above.
Results may differ from a plain program's by a relative error of at most 0.001.
Values may be sent and summed in bfloat16 or wider, within the bound.
No kernel may reach another device: no remote copies, remote signals or barrier semaphores. Data moves between devices by JAX's collectives and lax.ppermute only.
A program may use at most 192 MiB of HBM per device.

v0:
```python
import functools

import jax
import jax.numpy as jnp
from jax import lax
from jax.experimental import pallas as pl
from jax.experimental.pallas import tpu as pltpu
from jax.sharding import PartitionSpec as P


AT = 8
META = 16


VMEM = pl.BlockSpec(memory_space=pltpu.VMEM)
SMEM = pl.BlockSpec(memory_space=pltpu.SMEM)
ANY = pl.BlockSpec(memory_space=pl.ANY)
HBM = pl.BlockSpec(memory_space=pltpu.HBM)
NONE = 1 << 20


def swap(value, mask, sizes):
    rows, cols = sizes
    pairs = [
        (r * cols + c, (r ^ mask[0]) * cols + (c ^ mask[1]))
        for r in range(rows)
        for c in range(cols)
    ]
    return lax.ppermute(value, ("row", "col"), pairs)


def gather_all(block, tables, sizes):
    rows, cols = sizes
    step = cols // 4
    far = [(0, m * step) for m in range(4)]
    near = [(2 * i, j) for i in range(rows // 2) for j in range(step)]
    pieces = {0: block}
    for m in (3, 2, 1):
        pieces[m] = swap(block, far[m], sizes)
    line = jnp.concatenate([pieces[m] for m in range(4)], axis=0)
    line, tables = lax.optimization_barrier((line, tables))
    parts = [line]
    order = list(reversed(near[1:]))
    for mask in order:
        parts.append(swap(line, mask, sizes))
    mine = jnp.concatenate(parts, axis=0)
    other = swap(mine, (1, 0), sizes)
    return mine, other, tables


def gather_masks(sizes):
    rows, cols = sizes
    step = cols // 4
    far = [(0, m * step) for m in range(4)]
    near = [(2 * i, j) for i in range(rows // 2) for j in range(step)]
    masks = [near[0]] + list(reversed(near[1:]))
    held = [(a[0] ^ b[0], a[1] ^ b[1]) for a in masks for b in far]
    return held + [(a ^ 1, b) for a, b in held]


def contract_kernel(pair_rows, inner_tiles, unroll, source, tables, amp, mine, other, *rest):
    outs, total = rest[:-1], rest[-1]
    count = 2 * mine.shape[0]
    half = mine.shape[0]
    width = mine.shape[2]
    tiles = amp.shape[0] // pair_rows
    total[...] = jnp.zeros_like(total)

    def add_tiles(ref, base):
        def step(q, carry):
            k, a = tables[base + q], tables[count + base + q]
            inner = pl.ds(pl.multiple_of(k * width, width), width)
            outer = pl.ds(pl.multiple_of(a * width, width), width)
            parts = []
            for s in range(tiles):
                part = amp[s * pair_rows : (s + 1) * pair_rows, inner]
                alive = tables[2 * count + s * inner_tiles + k] != 0
                parts.append(jnp.where(alive, part, jnp.zeros_like(part)))
            left = jnp.concatenate(parts, axis=0)
            right = ref[q, pl.ds(0, width), :]
            total[:, outer] += jnp.dot(left, right, preferred_element_type=jnp.float32)
            return carry

        lax.fori_loop(0, half, step, 0, unroll=min(unroll, half))

    add_tiles(mine, 0)
    add_tiles(other, half)
    for n, out in enumerate(outs):
        start = pl.multiple_of(source[n] * pair_rows, pair_rows)
        out[...] = total[pl.ds(start, pair_rows), :].astype(out.dtype)


def contract(source, tables, amp, mine, other, count, pair_rows, inner_tiles):
    width = mine.shape[2]
    body = functools.partial(contract_kernel, pair_rows, inner_tiles, 16)
    return pl.pallas_call(
        body,
        out_shape=[jax.ShapeDtypeStruct((pair_rows, AT * width), amp.dtype)] * count,
        in_specs=[SMEM] * 2 + [VMEM] * 3,
        out_specs=[VMEM] * count,
        scratch_shapes=[pltpu.VMEM((amp.shape[0], AT * width), jnp.float32)],
        compiler_params=pltpu.CompilerParams(vmem_limit_bytes=40 * 1024 * 1024),
        name="contract",
    )(source, tables, amp, mine, other)


def destinations(block, width):
    told = block[pl.ds(width, META), :].astype(jnp.float32)
    return told[0:1], told[1:2]


def arrivals_kernel(slots, width, mine, positions, onward):
    my_col = lax.axis_index("col")
    told = [destinations(mine.at[q], width) for q in slots]
    column = jnp.concatenate([t[0] for t in told], axis=0).astype(jnp.int32)
    spot = jnp.concatenate([t[1] for t in told], axis=0).astype(jnp.int32)
    lane = lax.broadcasted_iota(jnp.int32, column.shape, 1)

    def landing(owner):
        match = column == owner
        first = jnp.min(jnp.where(match, lane, NONE), axis=1, keepdims=True)
        match = jnp.logical_and(match, lane != first)
        second = jnp.min(jnp.where(match, lane, NONE), axis=1, keepdims=True)

        def spot_at(at):
            found = jnp.sum(jnp.where(lane == at, spot, 0), axis=1, keepdims=True)
            return jnp.where(at < NONE, found, -1)

        return spot_at(first), spot_at(second)

    first, second = landing(my_col)
    _, passed = landing(my_col ^ 1)
    for m in range(len(slots)):
        positions[m] = first[m, 0]
        positions[len(slots) + m] = second[m, 0]
    chosen, odd = jnp.int32(0), jnp.int32(-1)
    for m in range(2, len(slots), 2):
        chosen = jnp.where(passed[m, 0] >= 0, m, chosen)
    for m in range(1, len(slots), 2):
        odd = jnp.maximum(odd, second[m, 0])
    onward[0] = chosen
    positions[2 * len(slots)] = odd


def arrivals(mine, slots, width):
    return pl.pallas_call(
        functools.partial(arrivals_kernel, slots, width),
        out_shape=[
            jax.ShapeDtypeStruct((2 * len(slots) + 1,), jnp.int32),
            jax.ShapeDtypeStruct((1,), jnp.int32),
        ],
        in_specs=[VMEM],
        out_specs=[SMEM, SMEM],
        name="arrivals",
    )(mine)


def crowding_kernel(groups, width, mine, other, crowded):
    my_col = lax.axis_index("col")
    half = mine.shape[0]
    worst = jnp.int32(0)
    for slots in groups:
        blocks = [(mine.at[q] if q < half else other.at[q - half]) for q in slots]
        column = jnp.concatenate([destinations(b, width)[0] for b in blocks], axis=0)
        column = column.astype(jnp.int32)
        lane = lax.broadcasted_iota(jnp.int32, column.shape, 1)
        owner = lax.broadcasted_iota(jnp.int32, column.shape, 0) ^ my_col
        spare = jnp.zeros(column.shape, jnp.int32)
        for d in range(len(slots)):
            count = jnp.sum((column == d).astype(jnp.int32), axis=1, keepdims=True)
            spare = jnp.where(lane == d, jnp.maximum(count - 1, 0), spare)
        spare = jnp.where(lane == owner, 0, spare)
        sent = jnp.max(jnp.sum(spare, axis=1, keepdims=True))
        taken = jnp.max(jnp.sum(spare, axis=0, keepdims=True))
        worst = jnp.maximum(worst, jnp.maximum(sent, taken))
    crowded[0] = worst


def crowding(mine, other, groups, width):
    return pl.pallas_call(
        functools.partial(crowding_kernel, groups, width),
        out_shape=jax.ShapeDtypeStruct((1,), jnp.int32),
        in_specs=[VMEM, VMEM],
        out_specs=SMEM,
        name="crowding",
    )(mine, other)


def choose_kernel(onward, *rest):
    choices, out, sem = rest[:-2], rest[-2], rest[-1]
    for n, choice in enumerate(choices):

        @pl.when(onward[0] == 2 * n)
        def _(choice=choice):
            copy = pltpu.make_async_copy(choice, out, sem)
            copy.start()
            copy.wait()


def choose(onward, choices):
    return pl.pallas_call(
        choose_kernel,
        out_shape=jax.ShapeDtypeStruct(choices[0].shape, choices[0].dtype),
        in_specs=[SMEM] + [ANY] * len(choices),
        out_specs=VMEM,
        scratch_shapes=[pltpu.SemaphoreType.DMA],
        name="choose",
    )(onward, *choices)


def place_kernel(places, positions, *rest):
    sources = rest[: len(places)]
    out, left = rest[-2:]
    rows = sources[0].shape[0]

    def store(n, source):
        start = pl.multiple_of(jnp.maximum(positions[places[n]], 0) * rows, rows)
        return pltpu.make_async_copy(source, out.at[pl.ds(start, rows), :], left.at[n])

    for n, source in enumerate(sources):
        pl.when(positions[places[n]] >= 0)(lambda n=n, source=source: store(n, source).start())
    for n, source in enumerate(sources):
        pl.when(positions[places[n]] >= 0)(lambda n=n, source=source: store(n, source).wait())


def place(places, positions, sources, tile_count, ladder=None):
    rows, width = sources[0].shape
    count = len(sources)
    into = [] if ladder is None else [ladder]
    return pl.pallas_call(
        functools.partial(place_kernel, places),
        out_shape=pltpu.HBM((tile_count * rows, width), sources[0].dtype),
        in_specs=[SMEM] + [VMEM] * count + [HBM] * len(into),
        out_specs=HBM,
        scratch_shapes=[pltpu.SemaphoreType.DMA((count,))],
        input_output_aliases={1 + count: 0} if into else {},
        name="place",
    )(positions, *sources, *into)


def nth(matches, n):
    size = matches.shape[-1]
    index = jnp.arange(size, dtype=jnp.int32)
    earlier = index[None, :] < index[:, None]
    rank = jnp.sum(jnp.logical_and(matches[..., None, :], earlier), axis=-1)
    chosen = jnp.logical_and(matches, rank == n)
    return jnp.sum(jnp.where(chosen, index, 0), axis=-1), jnp.any(chosen, axis=-1)


def shards(sizes, *arrays):
    return step(sizes, *arrays)


def hops(cols):
    high = [1 << b for b in reversed(range(1, cols.bit_length() - 1))]
    far = [(None, m) for m in reversed(range(high[0], cols))]
    near = [(None, m) for m in reversed(range(1, high[0]))]
    late, known = [], [0]
    for bit in high:
        late += [(m, bit) for m in known if m]
        known += [m | bit for m in known]
    early = [(0, bit) for bit in high] + near + far[:1]
    return early + late + far[1:]


def step(sizes, amplitudes, live_tiles, destination, integral_list, integral_tiles):
    rows, cols = sizes
    tile_count = destination.shape[0]
    pair_rows = amplitudes.shape[0] // tile_count
    inner_tiles = live_tiles.shape[1]
    held_tiles, width, _ = integral_tiles.shape
    my_row, my_col = lax.axis_index("row"), lax.axis_index("col")
    peers = jnp.arange(cols, dtype=jnp.int32)
    held = gather_masks(sizes)

    to_col = destination // tile_count % cols
    to_place = destination % tile_count
    meta = jnp.stack([to_col, to_place]).astype(integral_tiles.dtype)
    meta = jnp.pad(meta, ((0, META - 2), (0, width - tile_count)), constant_values=-1)
    meta = jnp.broadcast_to(meta[None], (held_tiles, META, width))
    block = jnp.concatenate([integral_tiles, meta], axis=1)

    matches = to_col[None, :] == (my_col ^ peers)[:, None]
    first, _ = nth(matches, 0)
    second, twice = nth(matches, 1)
    spare = jnp.logical_and(twice, peers > 0)
    extra = jnp.max(jnp.where(spare, second, 0))
    source = jnp.concatenate([first, second[:1], extra[None]])

    row_masks = jnp.array([m[0] for m in held], dtype=jnp.int32)
    col_masks = jnp.array([m[1] for m in held], dtype=jnp.int32)
    device_ids = (my_row ^ row_masks) * cols + (my_col ^ col_masks)
    entries = device_ids[:, None] * held_tiles + jnp.arange(held_tiles, dtype=jnp.int32)
    picked = integral_list[entries.reshape(-1)]
    tables = jnp.concatenate([picked[:, 0], picked[:, 1], live_tiles.reshape(-1)])

    mine, other, (source, tables) = gather_all(block, (source, tables), sizes)
    run = functools.partial(contract, pair_rows=pair_rows, inner_tiles=inner_tiles)
    outs = run(source, tables, amplitudes, mine, other, count=cols + 2)

    carried, direct = {0: outs[cols + 1]}, {}
    for hop in hops(cols):
        m, bit = hop
        if m is None:
            direct[bit] = swap(outs[bit], (0, bit), sizes)
        else:
            carried[m | bit] = swap(carried[m], (0, bit), sizes)

    index = {m: n * held_tiles for n, m in enumerate(held)}
    groups = [[index[(r, c)] for c in range(cols)] for r in range(rows)]
    positions, onward = arrivals(mine, groups[0], width)
    crowded = crowding(mine, other, groups, width)

    evens = list(range(2, cols, 2))
    last = choose(onward, [carried[0]] + [carried[m] for m in evens])
    last = swap(last, (0, 1), sizes)

    base = [outs[0]] + [direct[m] for m in range(1, cols)] + [outs[cols]]
    ladder = place(list(range(cols + 1)), positions, base, tile_count)
    spots = [cols + m for m in evens] + [2 * cols]
    ladder = place(spots, positions, [carried[m] for m in evens] + [last], tile_count, ladder)

    def again(state):
        return state[0] > 1

    def send_seconds(state):
        slots = run(second, tables, amplitudes, mine, other, count=cols)
        slots = [swap(slots[m], (0, m), sizes) for m in range(1, cols)]
        spots = list(range(cols + 1, 2 * cols))
        return jnp.zeros_like(state[0]), place(spots, positions, slots, tile_count, state[1])

    return lax.while_loop(again, send_seconds, (crowded[0], ladder))[1]


def solution(mesh):
    in_specs = (
        P(("row", "col"), None),
        P(("row", "col"), None),
        P(("row", "col")),
        P(),
        P(("row", "col"), None, None),
    )
    out_specs = P(("row", "col"), None)
    body = functools.partial(shards, (mesh.shape["row"], mesh.shape["col"]))
    return jax.shard_map(body, mesh=mesh, in_specs=in_specs, out_specs=out_specs, check_vma=False)
```

profile of v0, /device:TPU:10, one launch (start us, length us, event | category | flops | bytes accessed | tf_op | source)
XLA Modules:
  0.0 72.6 jit_solution(4731988374643448660)
XLA Ops:
  1.9 2.6 %collective-permute-start.8 = (bf16[1,144,128]{2,1,0:T(8,128)(2,1)S(1)}, bf16[1,144,128]{2,1,0:T(8,128)(2,1)S(1)}, u32[]{:S(2)}, u32[]{:S(2)}) collective-permute-start(bf16[1,144,128]{2,1,0:T(8,128)(2,1)S(1)} %pad_maximum_fusion.1), channel_id=1, source_target_pairs={{0,4},{1,5},{2,6},{3,7},{4,0},{5,1},{6,2},{7,3},{8,12},{9,13},{10,... | collective-permute-start | bytes 110600 | tf_op jit(solution)/shard_map/ppermute | solution.py:29
  10.9 1.6 %collective-permute-start.10 = (bf16[4,144,128]{2,1,0:T(8,128)(2,1)S(1)}, bf16[4,144,128]{2,1,0:T(8,128)(2,1)S(1)}, u32[]{:S(2)}, u32[]{:S(2)}) collective-permute-start(bf16[4,144,128]{2,1,0:T(8,128)(2,1)S(1)} %pad_maximum_fusion), channel_id=1, source_target_pairs={{0,17},{1,16},{2,19},{3,18},{4,21},{5,20},{6,23},{7,22},{8,25},{9,... | collective-permute-start | bytes 442376 | tf_op jit(solution)/shard_map/ppermute | solution.py:29
  12.5 1.5 %collective-permute-start.11 = (bf16[4,144,128]{2,1,0:T(8,128)(2,1)S(1)}, bf16[4,144,128]{2,1,0:T(8,128)(2,1)S(1)}, u32[]{:S(2)}, u32[]{:S(2)}) collective-permute-start(bf16[4,144,128]{2,1,0:T(8,128)(2,1)S(1)} %pad_maximum_fusion), channel_id=1, source_target_pairs={{0,16},{1,17},{2,18},{3,19},{4,20},{5,21},{6,22},{7,23},{8,24},{9,... | collective-permute-start | bytes 442376 | tf_op jit(solution)/shard_map/ppermute | solution.py:29
  14.6 3.8 %collective-permute-done.10 = bf16[4,144,128]{2,1,0:T(8,128)(2,1)S(1)} collective-permute-done((bf16[4,144,128]{2,1,0:T(8,128)(2,1)S(1)}, bf16[4,144,128]{2,1,0:T(8,128)(2,1)S(1)}, u32[]{:S(2)}, u32[]{:S(2)}) %collective-permute-start.10) | collective-permute-done | bytes 147488 | tf_op jit(solution)/shard_map/ppermute | solution.py:29
  18.3 1.5 %collective-permute-done.11 = bf16[4,144,128]{2,1,0:T(8,128)(2,1)S(1)} collective-permute-done((bf16[4,144,128]{2,1,0:T(8,128)(2,1)S(1)}, bf16[4,144,128]{2,1,0:T(8,128)(2,1)S(1)}, u32[]{:S(2)}, u32[]{:S(2)}) %collective-permute-start.11) | collective-permute-done | bytes 147488 | tf_op jit(solution)/shard_map/ppermute | solution.py:29
  20.0 2.0 %collective-permute-done.13.other = bf16[16,144,128]{2,1,0:T(8,128)(2,1)S(1)} collective-permute-done((bf16[16,144,128]{2,1,0:T(8,128)(2,1)S(1)}, bf16[16,144,128]{2,1,0:T(8,128)(2,1)S(1)}, u32[]{:S(2)}, u32[]{:S(2)}) %collective-permute-start.13) | collective-permute-done | bytes 589856 | tf_op jit(solution)/shard_map/ppermute | solution.py:29
  22.0 5.4 %contract.3 = (bf16[64,1024]{1,0:T(8,128)(2,1)S(1)}, bf16[64,1024]{1,0:T(8,128)(2,1)S(1)}, bf16[64,1024]{1,0:T(8,128)(2,1)S(1)}, bf16[64,1024]{1,0:T(8,128)(2,1)...) custom-call(s32[10]{0:T(128)S(1)} %pad_add_fusion.1.source, ...), custom_call_target="tpu_custom_call" | custom-call | tf_op jit(solution)/shard_map/contract/pallas_call | solution.py:96
  28.7 3.5 %collective-permute-start.15 = (bf16[64,1024]{1,0:T(8,128)(2,1)S(1)}, bf16[64,1024]{1,0:T(8,128)(2,1)S(1)}, u32[]{:S(2)}, u32[]{:S(2)}) collective-permute-start(bf16[64,1024]{1,0:T(8,128)(2,1)S(1)} %get-tuple-element.72.rest_0_), channel_id=1, source_target_pairs={{0,4},{1,5},{2,6},{3,7},{4,0},{5,1},{6,2},{7,3},{8,12},{9,13},{10,... | collective-permute-start | bytes 393224 | tf_op jit(solution)/shard_map/ppermute | solution.py:29
  32.2 1.4 %collective-permute-start.18 = (bf16[64,1024]{1,0:T(8,128)(2,1)S(1)}, bf16[64,1024]{1,0:T(8,128)(2,1)S(1)}, u32[]{:S(2)}, u32[]{:S(2)}) collective-permute-start(bf16[64,1024]{1,0:T(8,128)(2,1)S(1)} %get-tuple-element.75), channel_id=1, source_target_pairs={{0,1},{1,0},{2,3},{3,2},{4,5},{5,4},{6,7},{7,6},{8,9},{9,8},{10,11... | collective-permute-start | bytes 393224 | tf_op jit(solution)/shard_map/ppermute | solution.py:29
  33.6 2.0 %collective-permute-start.14 = (bf16[64,1024]{1,0:T(8,128)(2,1)S(1)}, bf16[64,1024]{1,0:T(8,128)(2,1)S(1)}, u32[]{:S(2)}, u32[]{:S(2)}) collective-permute-start(bf16[64,1024]{1,0:T(8,128)(2,1)S(1)} %get-tuple-element.72.rest_0_), channel_id=1, source_target_pairs={{0,2},{1,3},{2,0},{3,1},{4,6},{5,7},{6,4},{7,5},{8,10},{9,11},{10,... | collective-permute-start | bytes 393224 | tf_op jit(solution)/shard_map/ppermute | solution.py:29
  35.6 1.5 %collective-permute-done.15.rest_2_.rest_1_ = bf16[64,1024]{1,0:T(8,128)(2,1)S(1)} collective-permute-done((bf16[64,1024]{1,0:T(8,128)(2,1)S(1)}, bf16[64,1024]{1,0:T(8,128)(2,1)S(1)}, u32[]{:S(2)}, u32[]{:S(2)}) %collective-permute-start.15) | collective-permute-done | bytes 131104 | tf_op jit(solution)/shard_map/ppermute | solution.py:29
  37.0 2.4 %collective-permute-start.16 = (bf16[64,1024]{1,0:T(8,128)(2,1)S(1)}, bf16[64,1024]{1,0:T(8,128)(2,1)S(1)}, u32[]{:S(2)}, u32[]{:S(2)}) collective-permute-start(bf16[64,1024]{1,0:T(8,128)(2,1)S(1)} %collective-permute-done.15.rest_2_.rest_1_), channel_id=1, source_target_pairs={{0,2},{1,3},{2,0},{3,1},{4,6},{5,7},{6,4},{7,5},{8,10},{9,11},{10,... | collective-permute-start | bytes 393224 | tf_op jit(solution)/shard_map/ppermute | solution.py:29
  40.3 3.1 %collective-permute-start.21 = (bf16[64,1024]{1,0:T(8,128)(2,1)S(1)}, bf16[64,1024]{1,0:T(8,128)(2,1)S(1)}, u32[]{:S(2)}, u32[]{:S(2)}) collective-permute-start(bf16[64,1024]{1,0:T(8,128)(2,1)S(1)} %get-tuple-element.78), channel_id=1, source_target_pairs={{0,4},{1,5},{2,6},{3,7},{4,0},{5,1},{6,2},{7,3},{8,12},{9,13},{10,... | collective-permute-start | bytes 393224 | tf_op jit(solution)/shard_map/ppermute | solution.py:29
  43.5 1.4 %collective-permute-start.23 = (bf16[64,1024]{1,0:T(8,128)(2,1)S(1)}, bf16[64,1024]{1,0:T(8,128)(2,1)S(1)}, u32[]{:S(2)}, u32[]{:S(2)}) collective-permute-start(bf16[64,1024]{1,0:T(8,128)(2,1)S(1)} %get-tuple-element.80), channel_id=1, source_target_pairs={{0,6},{1,7},{2,4},{3,5},{4,2},{5,3},{6,0},{7,1},{8,14},{9,15},{10,... | collective-permute-start | bytes 393224 | tf_op jit(solution)/shard_map/ppermute | solution.py:29
  44.9 3.6 %collective-permute-done.16.rest_3_.rest_2_ = bf16[64,1024]{1,0:T(8,128)(2,1)S(1)} collective-permute-done((bf16[64,1024]{1,0:T(8,128)(2,1)S(1)}, bf16[64,1024]{1,0:T(8,128)(2,1)S(1)}, u32[]{:S(2)}, u32[]{:S(2)}) %collective-permute-start.16) | collective-permute-done | bytes 131104 | tf_op jit(solution)/shard_map/ppermute | solution.py:29
  49.2 1.0 %arrivals.1 = (s32[17]{0:T(128)S(1)}, s32[1]{0:T(128)}) custom-call(bf16[16,144,128]{2,1,0:T(8,128)(2,1)S(1)} %constant_dynamic-update-slice_fusion.mine), custom_call_target="tpu_custom_call" | custom-call | tf_op jit(solution)/shard_map/arrivals/pallas_call | solution.py:146
  50.3 2.2 %choose.1 = bf16[64,1024]{1,0:T(8,128)(2,1)} custom-call(s32[1]{0:T(128)} %get-tuple-element.73.onward, bf16[64,1024]{1,0:T(8,128)(2,1)} %copy-done.2, bf16[64,1024]{1,0:T(8,128)(2,1)} %copy-done.11, bf16[64,1024]{1,0:T(8,128)(2,1)} %copy-done.10, bf16[64,1024]{1,0:T(8,128)(2,1)} %copy-done.12), custom_call_target="tpu_custom_call" | custom-call | tf_op jit(solution)/shard_map/choose/pallas_call | solution.py:201
  52.6 1.6 %collective-permute-start.17 = (bf16[64,1024]{1,0:T(8,128)(2,1)}, bf16[64,1024]{1,0:T(8,128)(2,1)S(1)}, u32[]{:S(2)}, u32[]{:S(2)}) collective-permute-start(bf16[64,1024]{1,0:T(8,128)(2,1)} %choose.1), channel_id=1, source_target_pairs={{0,1},{1,0},{2,3},{3,2},{4,5},{5,4},{6,7},{7,6},{8,9},{9,8},{10,11... | collective-permute-start | bytes 393224 | tf_op jit(solution)/shard_map/ppermute | solution.py:29
  55.0 3.5 %collective-permute-done.21.rest_4_ = bf16[64,1024]{1,0:T(8,128)(2,1)S(1)} collective-permute-done((bf16[64,1024]{1,0:T(8,128)(2,1)S(1)}, bf16[64,1024]{1,0:T(8,128)(2,1)S(1)}, u32[]{:S(2)}, u32[]{:S(2)}) %collective-permute-start.21) | collective-permute-done | bytes 131104 | tf_op jit(solution)/shard_map/ppermute | solution.py:29
  58.5 2.8 %collective-permute-done.22.rest_5_ = bf16[64,1024]{1,0:T(8,128)(2,1)S(1)} collective-permute-done((bf16[64,1024]{1,0:T(8,128)(2,1)S(1)}, bf16[64,1024]{1,0:T(8,128)(2,1)S(1)}, u32[]{:S(2)}, u32[]{:S(2)}) %collective-permute-start.22) | collective-permute-done | bytes 131104 | tf_op jit(solution)/shard_map/ppermute | solution.py:29
  61.3 3.3 %collective-permute-done.23.rest_6_ = bf16[64,1024]{1,0:T(8,128)(2,1)S(1)} collective-permute-done((bf16[64,1024]{1,0:T(8,128)(2,1)S(1)}, bf16[64,1024]{1,0:T(8,128)(2,1)S(1)}, u32[]{:S(2)}, u32[]{:S(2)}) %collective-permute-start.23) | collective-permute-done | bytes 131104 | tf_op jit(solution)/shard_map/ppermute | solution.py:29
  64.6 1.8 %collective-permute-done.24.rest_7_ = bf16[64,1024]{1,0:T(8,128)(2,1)S(1)} collective-permute-done((bf16[64,1024]{1,0:T(8,128)(2,1)S(1)}, bf16[64,1024]{1,0:T(8,128)(2,1)S(1)}, u32[]{:S(2)}, u32[]{:S(2)}) %collective-permute-start.24) | collective-permute-done | bytes 131104 | tf_op jit(solution)/shard_map/ppermute | solution.py:29
  67.1 2.3 %place.4.rest_4_ = bf16[512,1024]{1,0:T(8,128)(2,1)} custom-call(s32[17]{0:T(128)S(1)} %get-tuple-element.123.positions, bf16[64,1024]{1,0:T(8,128)(2,1)} %copy-done, bf16[64,1024]{1,0:T(8,128)(2,1)} %copy-done.13, bf16[64,1024]{1,0:T(8,128)(2,1)} %copy-done.14, bf16[64,1024]{1,0:T(8,128)(2,1)} %copy-done.15, bf16[64,1024]{1,0:T(8,128)(2,1)} %copy-done.16, ...), custom_call_target="tpu_custom_call" | custom-call | tf_op jit(solution)/shard_map/place/pallas_call | solution.py:230
  70.2 1.8 %place.5 = bf16[512,1024]{1,0:T(8,128)(2,1)} custom-call(s32[17]{0:T(128)S(1)} %get-tuple-element.123.positions, bf16[64,1024]{1,0:T(8,128)(2,1)} %copy-done.11, bf16[64,1024]{1,0:T(8,128)(2,1)} %copy-done.10, bf16[64,1024]{1,0:T(8,128)(2,1)} %copy-done.12, bf16[64,1024]{1,0:T(8,128)(2,1)} %copy-done.20, ...), custom_call_target="tpu_custom_call", output_to_operand_aliasing={{}: (5, {})} | custom-call | tf_op jit(solution)/shard_map/place/pallas_call | solution.py:230
  (70 shorter events, 14.8 us)
Async XLA Ops:
  1.5 8.7 %collective-permute-start.7 = (bf16[1,144,128]{2,1,0:T(8,128)(2,1)S(1)}, bf16[1,144,128]{2,1,0:T(8,128)(2,1)S(1)}, u32[]{:S(2)}, u32[]{:S(2)}) collective-permute-start(bf16[1,144,128]{2,1,0:T(8,128)(2,1)S(1)} %pad_maximum_fusion.1), channel_id=1, source_target_pairs={{0,2},{1,3},{2,0},{3,1},{4,6},{5,7},{6,4},{7,5},{8,10},{9,11},{10,... | collective-permute-start | bytes 110600 | tf_op jit(solution)/shard_map/ppermute | solution.py:29
  1.9 8.2 %collective-permute-start.8 = (bf16[1,144,128]{2,1,0:T(8,128)(2,1)S(1)}, bf16[1,144,128]{2,1,0:T(8,128)(2,1)S(1)}, u32[]{:S(2)}, u32[]{:S(2)}) collective-permute-start(bf16[1,144,128]{2,1,0:T(8,128)(2,1)S(1)} %pad_maximum_fusion.1), channel_id=1, source_target_pairs={{0,4},{1,5},{2,6},{3,7},{4,0},{5,1},{6,2},{7,3},{8,12},{9,13},{10,... | collective-permute-start | bytes 110600 | tf_op jit(solution)/shard_map/ppermute | solution.py:29
  4.5 5.7 %collective-permute-start.9 = (bf16[1,144,128]{2,1,0:T(8,128)(2,1)S(1)}, bf16[1,144,128]{2,1,0:T(8,128)(2,1)S(1)}, u32[]{:S(2)}, u32[]{:S(2)}) collective-permute-start(bf16[1,144,128]{2,1,0:T(8,128)(2,1)S(1)} %pad_maximum_fusion.1), channel_id=1, source_target_pairs={{0,6},{1,7},{2,4},{3,5},{4,2},{5,3},{6,0},{7,1},{8,14},{9,15},{10,... | collective-permute-start | bytes 110600 | tf_op jit(solution)/shard_map/ppermute | solution.py:29
  10.9 7.4 %collective-permute-start.10 = (bf16[4,144,128]{2,1,0:T(8,128)(2,1)S(1)}, bf16[4,144,128]{2,1,0:T(8,128)(2,1)S(1)}, u32[]{:S(2)}, u32[]{:S(2)}) collective-permute-start(bf16[4,144,128]{2,1,0:T(8,128)(2,1)S(1)} %pad_maximum_fusion), channel_id=1, source_target_pairs={{0,17},{1,16},{2,19},{3,18},{4,21},{5,20},{6,23},{7,22},{8,25},{9,... | collective-permute-start | bytes 442376 | tf_op jit(solution)/shard_map/ppermute | solution.py:29
  12.5 7.4 %collective-permute-start.11 = (bf16[4,144,128]{2,1,0:T(8,128)(2,1)S(1)}, bf16[4,144,128]{2,1,0:T(8,128)(2,1)S(1)}, u32[]{:S(2)}, u32[]{:S(2)}) collective-permute-start(bf16[4,144,128]{2,1,0:T(8,128)(2,1)S(1)} %pad_maximum_fusion), channel_id=1, source_target_pairs={{0,16},{1,17},{2,18},{3,19},{4,20},{5,21},{6,22},{7,23},{8,24},{9,... | collective-permute-start | bytes 442376 | tf_op jit(solution)/shard_map/ppermute | solution.py:29
  14.0 5.9 %collective-permute-start.12 = (bf16[4,144,128]{2,1,0:T(8,128)(2,1)S(1)}, bf16[4,144,128]{2,1,0:T(8,128)(2,1)S(1)}, u32[]{:S(2)}, u32[]{:S(2)}) collective-permute-start(bf16[4,144,128]{2,1,0:T(8,128)(2,1)S(1)} %pad_maximum_fusion), channel_id=1, source_target_pairs={{0,1},{1,0},{2,3},{3,2},{4,5},{5,4},{6,7},{7,6},{8,9},{9,8},{10,11... | collective-permute-start | bytes 442376 | tf_op jit(solution)/shard_map/ppermute | solution.py:29
  19.9 2.1 %collective-permute-start.13 = (bf16[16,144,128]{2,1,0:T(8,128)(2,1)S(1)}, bf16[16,144,128]{2,1,0:T(8,128)(2,1)S(1)}, u32[]{:S(2)}, u32[]{:S(2)}) collective-permute-start(bf16[16,144,128]{2,1,0:T(8,128)(2,1)S(1)} %constant_dynamic-update-slice_fusion.mine), channel_id=1, source_target_pairs={{0,8},{1,9},{2,10},{3,11},{4,12},{5,13},{6,14},{7,15},{8,0},{9,1},... | collective-permute-start | bytes 1769480 | tf_op jit(solution)/shard_map/ppermute | solution.py:29
  28.7 21.6 %copy-start.2 = (bf16[64,1024]{1,0:T(8,128)(2,1)}, bf16[64,1024]{1,0:T(8,128)(2,1)S(1)}, u32[]{:S(2)}) copy-start(bf16[64,1024]{1,0:T(8,128)(2,1)S(1)} %get-tuple-element.72.rest_0_) | copy-start | bytes 393220
  28.7 8.4 %collective-permute-start.15 = (bf16[64,1024]{1,0:T(8,128)(2,1)S(1)}, bf16[64,1024]{1,0:T(8,128)(2,1)S(1)}, u32[]{:S(2)}, u32[]{:S(2)}) collective-permute-start(bf16[64,1024]{1,0:T(8,128)(2,1)S(1)} %get-tuple-element.72.rest_0_), channel_id=1, source_target_pairs={{0,4},{1,5},{2,6},{3,7},{4,0},{5,1},{6,2},{7,3},{8,12},{9,13},{10,... | collective-permute-start | bytes 393224 | tf_op jit(solution)/shard_map/ppermute | solution.py:29
  32.2 8.1 %collective-permute-start.18 = (bf16[64,1024]{1,0:T(8,128)(2,1)S(1)}, bf16[64,1024]{1,0:T(8,128)(2,1)S(1)}, u32[]{:S(2)}, u32[]{:S(2)}) collective-permute-start(bf16[64,1024]{1,0:T(8,128)(2,1)S(1)} %get-tuple-element.75), channel_id=1, source_target_pairs={{0,1},{1,0},{2,3},{3,2},{4,5},{5,4},{6,7},{7,6},{8,9},{9,8},{10,11... | collective-permute-start | bytes 393224 | tf_op jit(solution)/shard_map/ppermute | solution.py:29
  33.6 9.8 %collective-permute-start.19 = (bf16[64,1024]{1,0:T(8,128)(2,1)S(1)}, bf16[64,1024]{1,0:T(8,128)(2,1)S(1)}, u32[]{:S(2)}, u32[]{:S(2)}) collective-permute-start(bf16[64,1024]{1,0:T(8,128)(2,1)S(1)} %get-tuple-element.76), channel_id=1, source_target_pairs={{0,2},{1,3},{2,0},{3,1},{4,6},{5,7},{6,4},{7,5},{8,10},{9,11},{10,... | collective-permute-start | bytes 393224 | tf_op jit(solution)/shard_map/ppermute | solution.py:29
  33.6 9.9 %collective-permute-start.14 = (bf16[64,1024]{1,0:T(8,128)(2,1)S(1)}, bf16[64,1024]{1,0:T(8,128)(2,1)S(1)}, u32[]{:S(2)}, u32[]{:S(2)}) collective-permute-start(bf16[64,1024]{1,0:T(8,128)(2,1)S(1)} %get-tuple-element.72.rest_0_), channel_id=1, source_target_pairs={{0,2},{1,3},{2,0},{3,1},{4,6},{5,7},{6,4},{7,5},{8,10},{9,11},{10,... | collective-permute-start | bytes 393224 | tf_op jit(solution)/shard_map/ppermute | solution.py:29
  37.0 13.3 %copy-start.10 = (bf16[64,1024]{1,0:T(8,128)(2,1)}, bf16[64,1024]{1,0:T(8,128)(2,1)S(1)}, u32[]{:S(2)}) copy-start(bf16[64,1024]{1,0:T(8,128)(2,1)S(1)} %collective-permute-done.15.rest_2_.rest_1_) | copy-start | bytes 393220
  37.0 11.6 %collective-permute-start.16 = (bf16[64,1024]{1,0:T(8,128)(2,1)S(1)}, bf16[64,1024]{1,0:T(8,128)(2,1)S(1)}, u32[]{:S(2)}, u32[]{:S(2)}) collective-permute-start(bf16[64,1024]{1,0:T(8,128)(2,1)S(1)} %collective-permute-done.15.rest_2_.rest_1_), channel_id=1, source_target_pairs={{0,2},{1,3},{2,0},{3,1},{4,6},{5,7},{6,4},{7,5},{8,10},{9,11},{10,... | collective-permute-start | bytes 393224 | tf_op jit(solution)/shard_map/ppermute | solution.py:29
  39.4 13.1 %collective-permute-start.20 = (bf16[64,1024]{1,0:T(8,128)(2,1)S(1)}, bf16[64,1024]{1,0:T(8,128)(2,1)S(1)}, u32[]{:S(2)}, u32[]{:S(2)}) collective-permute-start(bf16[64,1024]{1,0:T(8,128)(2,1)S(1)} %get-tuple-element.77), channel_id=1, source_target_pairs={{0,3},{1,2},{2,1},{3,0},{4,7},{5,6},{6,5},{7,4},{8,11},{9,10},{10,... | collective-permute-start | bytes 393224 | tf_op jit(solution)/shard_map/ppermute | solution.py:29
  40.3 26.2 %copy-start.13 = (bf16[64,1024]{1,0:T(8,128)(2,1)}, bf16[64,1024]{1,0:T(8,128)(2,1)S(1)}, u32[]{:S(2)}) copy-start(bf16[64,1024]{1,0:T(8,128)(2,1)S(1)} %collective-permute-done.18.rest_1_) | copy-start | bytes 393220
  40.3 18.2 %collective-permute-start.21 = (bf16[64,1024]{1,0:T(8,128)(2,1)S(1)}, bf16[64,1024]{1,0:T(8,128)(2,1)S(1)}, u32[]{:S(2)}, u32[]{:S(2)}) collective-permute-start(bf16[64,1024]{1,0:T(8,128)(2,1)S(1)} %get-tuple-element.78), channel_id=1, source_target_pairs={{0,4},{1,5},{2,6},{3,7},{4,0},{5,1},{6,2},{7,3},{8,12},{9,13},{10,... | collective-permute-start | bytes 393224 | tf_op jit(solution)/shard_map/ppermute | solution.py:29
  43.4 23.1 %copy-start.14 = (bf16[64,1024]{1,0:T(8,128)(2,1)}, bf16[64,1024]{1,0:T(8,128)(2,1)S(1)}, u32[]{:S(2)}) copy-start(bf16[64,1024]{1,0:T(8,128)(2,1)S(1)} %collective-permute-done.19.rest_2_) | copy-start | bytes 393220
  43.4 17.9 %collective-permute-start.22 = (bf16[64,1024]{1,0:T(8,128)(2,1)S(1)}, bf16[64,1024]{1,0:T(8,128)(2,1)S(1)}, u32[]{:S(2)}, u32[]{:S(2)}) collective-permute-start(bf16[64,1024]{1,0:T(8,128)(2,1)S(1)} %get-tuple-element.79), channel_id=1, source_target_pairs={{0,5},{1,4},{2,7},{3,6},{4,1},{5,0},{6,3},{7,2},{8,13},{9,12},{10,... | collective-permute-start | bytes 393224 | tf_op jit(solution)/shard_map/ppermute | solution.py:29
  43.5 21.1 %collective-permute-start.23 = (bf16[64,1024]{1,0:T(8,128)(2,1)S(1)}, bf16[64,1024]{1,0:T(8,128)(2,1)S(1)}, u32[]{:S(2)}, u32[]{:S(2)}) collective-permute-start(bf16[64,1024]{1,0:T(8,128)(2,1)S(1)} %get-tuple-element.80), channel_id=1, source_target_pairs={{0,6},{1,7},{2,4},{3,5},{4,2},{5,3},{6,0},{7,1},{8,14},{9,15},{10,... | collective-permute-start | bytes 393224 | tf_op jit(solution)/shard_map/ppermute | solution.py:29
  48.6 17.9 %collective-permute-start.24 = (bf16[64,1024]{1,0:T(8,128)(2,1)S(1)}, bf16[64,1024]{1,0:T(8,128)(2,1)S(1)}, u32[]{:S(2)}, u32[]{:S(2)}) collective-permute-start(bf16[64,1024]{1,0:T(8,128)(2,1)S(1)} %get-tuple-element.81), channel_id=1, source_target_pairs={{0,7},{1,6},{2,5},{3,4},{4,3},{5,2},{6,1},{7,0},{8,15},{9,14},{10,... | collective-permute-start | bytes 393224 | tf_op jit(solution)/shard_map/ppermute | solution.py:29
  52.6 13.9 %copy-start.15 = (bf16[64,1024]{1,0:T(8,128)(2,1)}, bf16[64,1024]{1,0:T(8,128)(2,1)S(1)}, u32[]{:S(2)}) copy-start(bf16[64,1024]{1,0:T(8,128)(2,1)S(1)} %collective-permute-done.20.rest_3_) | copy-start | bytes 393220
  52.6 16.9 %collective-permute-start.17 = (bf16[64,1024]{1,0:T(8,128)(2,1)}, bf16[64,1024]{1,0:T(8,128)(2,1)S(1)}, u32[]{:S(2)}, u32[]{:S(2)}) collective-permute-start(bf16[64,1024]{1,0:T(8,128)(2,1)} %choose.1), channel_id=1, source_target_pairs={{0,1},{1,0},{2,3},{3,2},{4,5},{5,4},{6,7},{7,6},{8,9},{9,8},{10,11... | collective-permute-start | bytes 393224 | tf_op jit(solution)/shard_map/ppermute | solution.py:29
  58.5 8.0 %copy-start.16 = (bf16[64,1024]{1,0:T(8,128)(2,1)}, bf16[64,1024]{1,0:T(8,128)(2,1)S(1)}, u32[]{:S(2)}) copy-start(bf16[64,1024]{1,0:T(8,128)(2,1)S(1)} %collective-permute-done.21.rest_4_) | copy-start | bytes 393220
  (8 other events, 18.2 us)
where the time goes:
time: 73 us; the launch traced here: 72.6 us
  starting transfers between devices  24.2 us (33%)
  waiting for transfers between devices  23.8 us (33%)
  Pallas kernels  13.6 us (19%)
  other arithmetic  5.13 us (7%)
  local copies, waits for them, and re-layouts  4.97 us (7%)
    ppermute x18, starting transfers between devices, swap(): return lax.ppermute(value, ('row', 'col'), pairs)  24.2 us
    ppermute x18, waiting for transfers between devices, swap(): return lax.ppermute(value, ('row', 'col'), pairs)  23.8 us
    pallas_call x1, Pallas kernels, contract(): pl.pallas_call(body, out_shape=[jax.ShapeDtypeStruct((pair_rows, AT * wid...  5.35 us
    pallas_call x2, Pallas kernels, place(): pl.pallas_call(functools.partial(place_kernel, places), out_shape=pltpu.H...  4.13 us
    unnamed x32, local copies, waits for them, and re-layouts  3.43 us
    pallas_call x1, Pallas kernels, choose(): pl.pallas_call(choose_kernel, out_shape=jax.ShapeDtypeStruct(choices[0].s...  2.21 us
  transfers between devices with their start and end apart: 18, of which 9 were waited for; matrix products, arithmetic and copies ran while one was open for 7% of the time, Pallas kernels for 9%

commit v1 on v0

v1 whole, which is shorter than its diff:
```python
import functools

import jax
import jax.numpy as jnp
from jax import lax
from jax.experimental import pallas as pl
from jax.experimental.pallas import tpu as pltpu
from jax.sharding import PartitionSpec as P


AT = 8
META = 16


GRANT = pltpu.CompilerParams(vmem_limit_bytes=40 * 1024 * 1024)
SMALL = pltpu.CompilerParams(vmem_limit_bytes=12 * 1024 * 1024)
VMEM = pl.BlockSpec(memory_space=pltpu.VMEM)
SMEM = pl.BlockSpec(memory_space=pltpu.SMEM)
ANY = pl.BlockSpec(memory_space=pl.ANY)
HBM = pl.BlockSpec(memory_space=pltpu.HBM)
NONE = 1 << 20
LAST = (None, None)


def swap(value, mask, sizes):
    rows, cols = sizes
    pairs = [
        (r * cols + c, (r ^ mask[0]) * cols + (c ^ mask[1]))
        for r in range(rows)
        for c in range(cols)
    ]
    return lax.ppermute(value, ("row", "col"), pairs)


def local(value):
    return pltpu.with_memory_space_constraint(value, pltpu.VMEM)


def join_kernel(*refs):
    out = refs[-1]
    size = refs[0].shape[0]
    for n, ref in enumerate(refs[:-1]):
        out[n * size : (n + 1) * size] = ref[...]


def join(pieces):
    shape = pieces[0].shape
    return pl.pallas_call(
        join_kernel,
        out_shape=pltpu.VMEM((len(pieces) * shape[0], *shape[1:]), pieces[0].dtype),
        in_specs=[VMEM] * len(pieces),
        out_specs=VMEM,
        compiler_params=SMALL,
        name="join",
    )(*[local(piece) for piece in pieces])


def gather_all(block, sizes):
    rows, cols = sizes
    step = cols // 4
    near = [(2 * i, j) for i in range(rows // 2) for j in range(step)]
    pieces = {0: block}
    for m in (3, 2, 1):
        pieces[m] = swap(block, (0, m * step), sizes)
    line = join([pieces[m] for m in range(4)])
    mine, other = {0: line}, {}
    for n in reversed(range(1, len(near))):
        mine[n] = swap(line, near[n], sizes)
    for n in range(len(near)):
        other[n] = swap(mine[n], (1, 0), sizes)
    count = range(len(near))
    return [local(mine[n]) for n in count], [local(other[n]) for n in count]


def gather_mask(q, half, cols):
    step = cols // 4
    line, far = divmod(q, 4)
    return 2 * (line // step) + half, line % step + far * step


def mask_kernel(pair_rows, width, live, amp, out, sems):
    tiles = amp.shape[0] // pair_rows

    def fetch(s):
        rows = pl.ds(s * pair_rows, pair_rows)
        return pltpu.make_async_copy(amp.at[rows, :], out.at[rows, :], sems.at[s])

    for s in range(tiles):
        fetch(s).start()
    for s in range(tiles):
        fetch(s).wait()
        for k in range(amp.shape[1] // width):
            part = out[s * pair_rows : (s + 1) * pair_rows, k * width : (k + 1) * width]
            part = jnp.where(live[s, k] != 0, part, jnp.zeros_like(part))
            out[s * pair_rows : (s + 1) * pair_rows, k * width : (k + 1) * width] = part


def mask_amplitudes(live, amp, pair_rows, width):
    tiles = amp.shape[0] // pair_rows
    return pl.pallas_call(
        functools.partial(mask_kernel, pair_rows, width),
        out_shape=pltpu.VMEM(amp.shape, amp.dtype),
        in_specs=[SMEM, HBM],
        out_specs=VMEM,
        scratch_shapes=[pltpu.SemaphoreType.DMA((tiles,))],
        compiler_params=SMALL,
        name="mask",
    )(live, pltpu.with_memory_space_constraint(amp, pltpu.HBM))


def add_tiles(places, total, refs, half, held_tiles, cols, rows):
    my_row, my_col = lax.axis_index("row"), lax.axis_index("col")
    base, step = places_at(cols), cols // 4

    def add(ref, line, q):
        width = ref.shape[2]
        far = q // held_tiles
        row_mask, col_mask = 2 * (line // step) + half, line % step + far * step
        entry = ((my_row ^ row_mask) * cols + (my_col ^ col_mask)) * held_tiles + q % held_tiles
        k, a = places[base + 2 * entry], places[base + 2 * entry + 1]
        inner = pl.ds(pl.multiple_of(k * width, width), width)
        outer = pl.ds(pl.multiple_of(a * width, width), width)
        right = ref[q, pl.ds(0, width), :]
        total[:, outer] += jnp.dot(rows(inner), right, preferred_element_type=jnp.float32)

    for line, ref in enumerate(refs):
        for q in range(ref.shape[0]):
            add(ref, line, q)


def contract_mine_kernel(held_tiles, cols, table, amp, *rest):
    mine, total = rest[:-1], rest[-1]
    total[...] = jnp.zeros_like(total)
    add_tiles(table, total, mine, 0, held_tiles, cols, lambda inner: amp[:, inner])


def contract_one_kernel(slot, pair_rows, held_tiles, cols, table, amp, given, *rest):
    other, (out, _, one) = rest[:-3], rest[-3:]
    picked = pl.ds(pl.multiple_of(table[slot] * pair_rows, pair_rows), pair_rows)
    one[...] = given[picked, :]
    add_tiles(table, one, other, 1, held_tiles, cols, lambda inner: amp[picked, inner])
    out[...] = one[...].astype(out.dtype)


def contract_rest_kernel(slots, own, parts, pair_rows, held_tiles, cols, table, amp, given, *rest):
    other, rest = rest[:parts], rest[parts:]
    outs = rest[: len(slots)]
    if own:
        total, ladder, kept, sems = rest[len(slots) :]
    else:
        (total,) = rest[len(slots) :]
    add_tiles(table, total, other, 1, held_tiles, cols, lambda inner: amp[:, inner])

    def product(slot):
        start = pl.multiple_of(table[slot] * pair_rows, pair_rows)
        return total[pl.ds(start, pair_rows), :]

    copies = []
    for n, (slot, where) in enumerate(own):
        start = pl.multiple_of(jnp.maximum(table[where], 0) * pair_rows, pair_rows)
        kept[n] = product(slot).astype(kept.dtype)
        copy = pltpu.make_async_copy(kept.at[n], ladder.at[pl.ds(start, pair_rows), :], sems.at[n])
        copies.append((table[where] >= 0, copy))
        pl.when(table[where] >= 0)(copy.start)
    for slot, out in zip(slots, outs):
        out[...] = product(slot).astype(out.dtype)
    for there, copy in copies:
        pl.when(there)(copy.wait)


def contract_mine(table, amp, mine, sizes):
    return pl.pallas_call(
        functools.partial(contract_mine_kernel, *sizes[1:]),
        out_shape=pltpu.VMEM((amp.shape[0], AT * mine[0].shape[2]), jnp.float32),
        in_specs=[SMEM, VMEM] + [VMEM] * len(mine),
        out_specs=VMEM,
        compiler_params=GRANT,
        name="contract_mine",
    )(table, amp, *mine)


def contract_one(slot, table, amp, other, total, sizes):
    shape = (sizes[0], total.shape[1])
    return pl.pallas_call(
        functools.partial(contract_one_kernel, slot, *sizes),
        out_shape=[pltpu.VMEM(shape, amp.dtype), pltpu.VMEM(total.shape, total.dtype)],
        in_specs=[SMEM, VMEM, VMEM] + [VMEM] * len(other),
        out_specs=[VMEM, VMEM],
        scratch_shapes=[pltpu.VMEM(shape, jnp.float32)],
        input_output_aliases={2: 1},
        compiler_params=GRANT,
        name="contract_one",
    )(table, amp, total, *other)


def contract_rest(slots, own, table, amp, other, total, sizes):
    shape = (sizes[0], total.shape[1])
    out_shape = [pltpu.VMEM(shape, amp.dtype)] * len(slots)
    out_shape.append(pltpu.VMEM(total.shape, total.dtype))
    scratch = []
    if own:
        out_shape.append(pltpu.HBM(total.shape, amp.dtype))
        scratch = [pltpu.VMEM((len(own), *shape), amp.dtype), pltpu.SemaphoreType.DMA((len(own),))]
    return pl.pallas_call(
        functools.partial(contract_rest_kernel, slots, own, len(other), *sizes),
        out_shape=out_shape,
        in_specs=[SMEM, VMEM, VMEM] + [VMEM] * len(other),
        out_specs=[VMEM] * (len(slots) + 1) + [HBM] * (1 if own else 0),
        scratch_shapes=scratch,
        input_output_aliases={2: len(slots)},
        compiler_params=GRANT,
        name="contract_rest",
    )(table, amp, total, *other)


def places_at(cols):
    return 3 * cols + 4


def table_kernel(cols, destination, integrals, table):
    my_col = lax.axis_index("col")
    count = destination.shape[0]
    again, seen_at, base = cols + 4, 2 * cols + 4, places_at(cols)
    for n in range(base):
        table[n] = 0
    table[cols + 2] = -1
    table[cols + 3] = -1
    for s in range(count):
        mask = destination[s] // count % cols ^ my_col
        spot = destination[s] % count
        seen = table[seen_at + mask]
        table[seen_at + mask] = seen + 1

        @pl.when(seen == 0)
        def _(s=s, mask=mask):
            table[mask] = s

        @pl.when(seen > 0)
        def _(s=s, mask=mask):
            table[again + mask] = s

        @pl.when(mask == 0)
        def _(s=s, seen=seen, spot=spot):
            table[cols + 2 + jnp.minimum(seen, 1)] = spot

        @pl.when(jnp.logical_and(mask == 0, seen > 0))
        def _(s=s):
            table[cols] = s

        @pl.when(jnp.logical_and(mask != 0, seen > 0))
        def _(s=s):
            table[cols + 1] = s

    for n in range(integrals.shape[0]):
        table[base + 2 * n] = integrals[n, 0]
        table[base + 2 * n + 1] = integrals[n, 1]


def make_table(destination, integrals, cols):
    size = places_at(cols) + 2 * integrals.shape[0]
    return pl.pallas_call(
        functools.partial(table_kernel, cols),
        out_shape=pltpu.SMEM((size,), jnp.int32),
        in_specs=[SMEM, SMEM],
        out_specs=SMEM,
        compiler_params=SMALL,
        name="table",
    )(destination, integrals)


def destinations(block, width):
    told = block[pl.ds(width, META), :].astype(jnp.float32)
    return told[0:1], told[1:2]


def arrivals_kernel(slots, width, *refs):
    my_col = lax.axis_index("col")
    mine, (positions, onward) = refs[:-2], refs[-2:]
    told = [destinations(mine[n].at[q], width) for n, q in slots]
    column = jnp.concatenate([t[0] for t in told], axis=0).astype(jnp.int32)
    spot = jnp.concatenate([t[1] for t in told], axis=0).astype(jnp.int32)
    lane = lax.broadcasted_iota(jnp.int32, column.shape, 1)

    def landing(owner):
        match = column == owner
        first = jnp.min(jnp.where(match, lane, NONE), axis=1, keepdims=True)
        match = jnp.logical_and(match, lane != first)
        second = jnp.min(jnp.where(match, lane, NONE), axis=1, keepdims=True)

        def spot_at(at):
            found = jnp.sum(jnp.where(lane == at, spot, 0), axis=1, keepdims=True)
            return jnp.where(at < NONE, found, -1)

        return spot_at(first), spot_at(second)

    first, second = landing(my_col)
    _, passed = landing(my_col ^ 1)
    for m in range(len(slots)):
        positions[m] = first[m, 0]
        positions[len(slots) + m] = second[m, 0]
    chosen, odd = jnp.int32(0), jnp.int32(-1)
    for m in range(2, len(slots), 2):
        chosen = jnp.where(passed[m, 0] >= 0, m, chosen)
    for m in range(1, len(slots), 2):
        odd = jnp.maximum(odd, second[m, 0])
    onward[0] = chosen
    positions[2 * len(slots)] = odd


def arrivals(mine, slots, width):
    return pl.pallas_call(
        functools.partial(arrivals_kernel, slots, width),
        out_shape=[
            pltpu.SMEM((2 * len(slots) + 1,), jnp.int32),
            pltpu.SMEM((1,), jnp.int32),
        ],
        in_specs=[VMEM] * len(mine),
        out_specs=[SMEM, SMEM],
        compiler_params=SMALL,
        name="arrivals",
    )(*mine)


def crowding_kernel(groups, width, *refs):
    my_col = lax.axis_index("col")
    refs, crowded = refs[:-1], refs[-1]
    worst = jnp.int32(0)
    for slots in groups:
        blocks = [refs[n].at[q] for n, q in slots]
        column = jnp.concatenate([destinations(b, width)[0] for b in blocks], axis=0)
        column = column.astype(jnp.int32)
        lane = lax.broadcasted_iota(jnp.int32, column.shape, 1)
        owner = lax.broadcasted_iota(jnp.int32, column.shape, 0) ^ my_col
        spare = jnp.zeros(column.shape, jnp.int32)
        for d in range(len(slots)):
            count = jnp.sum((column == d).astype(jnp.int32), axis=1, keepdims=True)
            spare = jnp.where(lane == d, jnp.maximum(count - 1, 0), spare)
        spare = jnp.where(lane == owner, 0, spare)
        sent = jnp.max(jnp.sum(spare, axis=1, keepdims=True))
        taken = jnp.max(jnp.sum(spare, axis=0, keepdims=True))
        worst = jnp.maximum(worst, jnp.maximum(sent, taken))
    crowded[0] = worst


def crowding(blocks, groups, width):
    return pl.pallas_call(
        functools.partial(crowding_kernel, groups, width),
        out_shape=jax.ShapeDtypeStruct((1,), jnp.int32),
        in_specs=[VMEM] * len(blocks),
        out_specs=SMEM,
        compiler_params=SMALL,
        name="crowding",
    )(*blocks)


def choose_kernel(onward, *rest):
    choices, out = rest[:-1], rest[-1]
    for n, choice in enumerate(choices):

        @pl.when(onward[0] == 2 * n)
        def _(choice=choice):
            out[...] = choice[...]


def choose(onward, choices):
    return pl.pallas_call(
        choose_kernel,
        out_shape=pltpu.VMEM(choices[0].shape, choices[0].dtype),
        in_specs=[SMEM] + [VMEM] * len(choices),
        out_specs=VMEM,
        compiler_params=SMALL,
        name="choose",
    )(onward, *choices)


def place_kernel(places, guarded, crowded, positions, *rest):
    sources = rest[: len(places)]
    out, left = rest[-2:]
    rows = sources[0].shape[0]

    def there(n):
        here = positions[places[n]] >= 0
        return jnp.logical_and(here, crowded[0] <= 1) if places[n] == guarded else here

    def store(n):
        start = pl.multiple_of(jnp.maximum(positions[places[n]], 0) * rows, rows)
        return pltpu.make_async_copy(sources[n], out.at[pl.ds(start, rows), :], left.at[n])

    for n in range(len(places)):
        pl.when(there(n))(lambda n=n: store(n).start())
    for n in range(len(places)):
        pl.when(there(n))(lambda n=n: store(n).wait())


def place(places, crowded, positions, sources, ladder, guarded=None):
    count = len(sources)
    return pl.pallas_call(
        functools.partial(place_kernel, places, guarded),
        out_shape=pltpu.HBM(ladder.shape, ladder.dtype),
        in_specs=[SMEM, SMEM] + [VMEM] * count + [HBM],
        out_specs=HBM,
        scratch_shapes=[pltpu.SemaphoreType.DMA((count,))],
        input_output_aliases={2 + count: 0},
        compiler_params=SMALL,
        name="place",
    )(crowded, positions, *sources, ladder)


def shards(sizes, *arrays):
    return step(sizes, *arrays)


def make_block(destination, integral_tiles, cols):
    tile_count = destination.shape[0]
    held_tiles, width, _ = integral_tiles.shape
    to_col = destination // tile_count % cols
    to_place = destination % tile_count
    meta = jnp.stack([to_col, to_place]).astype(integral_tiles.dtype)
    meta = jnp.pad(meta, ((0, META - 2), (0, width - tile_count)), constant_values=-1)
    meta = jnp.broadcast_to(meta[None], (held_tiles, META, width))
    return jnp.concatenate([integral_tiles, meta], axis=1)


def hops(cols):
    high = [1 << b for b in reversed(range(1, cols.bit_length() - 1))]
    far = [(None, m) for m in reversed(range(high[0], cols))]
    near = [(None, m) for m in reversed(range(1, high[0]))]
    late, known = [], [0]
    for bit in high:
        late += [(m, bit) for m in known if m]
        known += [m | bit for m in known]
    order = [(0, bit) for bit in high] + far[:1] + near[-1:] + late
    rest = []
    for n, hop in enumerate(far[1:]):
        rest += [hop] + near[:-1][n : n + 1]
    return order + rest[:-1] + [LAST] + rest[-1:]


def step(sizes, amplitudes, live_tiles, destination, integral_list, integral_tiles):
    rows, cols = sizes
    tile_count = destination.shape[0]
    pair_rows = amplitudes.shape[0] // tile_count
    held_tiles, width, _ = integral_tiles.shape
    block = make_block(destination, integral_tiles, cols)
    masked = mask_amplitudes(live_tiles, amplitudes, pair_rows, width)
    mine, other = gather_all(block, sizes)
    table = make_table(destination, integral_list, cols)
    shape = (pair_rows, held_tiles, cols)
    total = contract_mine(table, masked, mine, shape)
    extra_tile, total = contract_one(cols + 1, table, masked, other, total, shape)
    slots = list(range(1, cols))
    own = [(0, cols + 2), (cols, cols + 3)]
    *outs, _, ladder = contract_rest(slots, own, table, masked, other, total, shape)

    held = [gather_mask(q, half, cols) for half in (0, 1) for q in range(rows * cols // 2)]
    index = {m: (n // 4, n % 4 * held_tiles) for n, m in enumerate(held)}
    groups = [[index[(r, c)] for c in range(cols)] for r in range(rows)]
    positions, onward = arrivals(mine, groups[0], width)
    crowded = crowding(mine + other, groups, width)

    evens = list(range(2, cols, 2))
    carried, direct = {0: extra_tile}, {}
    for hop in hops(cols):
        m, bit = hop
        if hop == LAST:
            last = choose(onward, [carried[0]] + [carried[m] for m in evens])
            last = local(swap(last, (0, 1), sizes))
        elif m is None:
            direct[bit] = local(swap(outs[bit - 1], (0, bit), sizes))
        else:
            carried[m | bit] = local(swap(carried[m], (0, bit), sizes))

    soon, late = list(range(1, cols // 2)), list(range(cols // 2, cols))
    soon, late = soon + late[-2:], late[:-2]
    spots = soon + [cols + m for m in evens]
    sources = [direct[m] for m in soon] + [carried[m] for m in evens]
    ladder = place(spots, crowded, positions, sources, ladder)

    def again(state):
        return state[0] > 1

    def send_seconds(state):
        mine, other = gather_all(make_block(destination, integral_tiles, cols), sizes)
        table = make_table(destination, integral_list, cols)
        masked = mask_amplitudes(live_tiles, amplitudes, pair_rows, width)
        total = contract_mine(table, masked, mine, shape)
        again = [cols + 4 + m for m in slots]
        *outs, _ = contract_rest(again, [], table, masked, other, total, shape)
        outs = [local(swap(out, (0, m), sizes)) for m, out in zip(slots, outs)]
        spots = list(range(cols + 1, 2 * cols))
        return jnp.zeros_like(state[0]), place(spots, crowded, positions, outs, state[1])

    ladder = lax.while_loop(again, send_seconds, (crowded[0], ladder))[1]

    sources = [direct[m] for m in late] + [last]
    return place(late + [2 * cols], crowded, positions, sources, ladder, 2 * cols)


def solution(mesh):
    in_specs = (
        P(("row", "col"), None),
        P(("row", "col"), None),
        P(("row", "col")),
        P(),
        P(("row", "col"), None, None),
    )
    out_specs = P(("row", "col"), None)
    body = functools.partial(shards, (mesh.shape["row"], mesh.shape["col"]))
    return jax.shard_map(body, mesh=mesh, in_specs=in_specs, out_specs=out_specs, check_vma=False)
```

time: 73 us -> 69.7 us (0.955)
  the two profiles are of different devices: /device:TPU:10 before, /device:TPU:0 now
where the time goes in v1:
time: 69.7 us; the launch traced here: 69.4 us
  waiting for transfers between devices  29.7 us (43%)
  starting transfers between devices  24.8 us (36%)
  Pallas kernels  11.8 us (17%)
  other arithmetic  1.45 us (2%)
  between operations  0.82 us (1%)
  local copies, waits for them, and re-layouts  0.78 us (1%)
    ppermute x21, waiting for transfers between devices, swap(): return lax.ppermute(value, ('row', 'col'), pairs)  29.7 us
    ppermute x21, starting transfers between devices, swap(): return lax.ppermute(value, ('row', 'col'), pairs)  24.8 us
    pallas_call x1, Pallas kernels, mask_amplitudes(): pl.pallas_call(functools.partial(mask_kernel, pair_rows, width), out_shap...  3.07 us
    pallas_call x2, Pallas kernels, place(): pl.pallas_call(functools.partial(place_kernel, places, guarded), out_shap...  2.95 us
    pallas_call x1, Pallas kernels, contract_rest(): pl.pallas_call(functools.partial(contract_rest_kernel, slots, own, len(ot...  1.6 us
    pallas_call x1, Pallas kernels, contract_mine(): pl.pallas_call(functools.partial(contract_mine_kernel, *sizes[1:]), out_s...  1.54 us
  transfers between devices with their start and end apart: 21, of which 10 were waited for; matrix products, arithmetic and copies ran while one was open for 1% of the time, Pallas kernels for 10%

profile of v1, /device:TPU:0, one launch (start us, length us, event | category | flops | bytes accessed | tf_op | source)
XLA Modules:
  0.0 69.4 jit_solution(16304253767620247952)
XLA Ops:
  1.5 5.1 %collective-permute-start.19 = (bf16[1,144,128]{2,1,0:T(8,128)(2,1)S(1)}, bf16[1,144,128]{2,1,0:T(8,128)(2,1)S(1)}, u32[]{:S(2)}, u32[]{:S(2)}) collective-permute-start(bf16[1,144,128]{2,1,0:T(8,128)(2,1)S(1)} %pad_maximum_fusion.1.refs_0_), channel_id=1, source_target_pairs={{0,6},{1,7},{2,4},{3,5},{4,2},{5,3},{6,0},{7,1},{8,14},{9,15},{10,... | collective-permute-start | bytes 110600 | tf_op jit(solution)/shard_map/ppermute | solution.py:32
  7.1 1.4 %collective-permute-done.19.refs_3_ = bf16[1,144,128]{2,1,0:T(8,128)(2,1)S(1)} collective-permute-done((bf16[1,144,128]{2,1,0:T(8,128)(2,1)S(1)}, bf16[1,144,128]{2,1,0:T(8,128)(2,1)S(1)}, u32[]{:S(2)}, u32[]{:S(2)}) %collective-permute-start.19) | collective-permute-done | bytes 36896 | tf_op jit(solution)/shard_map/ppermute | solution.py:32
  8.5 2.9 %collective-permute-done.18.refs_2_ = bf16[1,144,128]{2,1,0:T(8,128)(2,1)S(1)} collective-permute-done((bf16[1,144,128]{2,1,0:T(8,128)(2,1)S(1)}, bf16[1,144,128]{2,1,0:T(8,128)(2,1)S(1)}, u32[]{:S(2)}, u32[]{:S(2)}) %collective-permute-start.18) | collective-permute-done | bytes 36896 | tf_op jit(solution)/shard_map/ppermute | solution.py:32
  11.4 2.5 %collective-permute-start.22 = (bf16[4,144,128]{2,1,0:T(8,128)(2,1)S(1)}, bf16[4,144,128]{2,1,0:T(8,128)(2,1)S(1)}, u32[]{:S(2)}, u32[]{:S(2)}) collective-permute-start(bf16[4,144,128]{2,1,0:T(8,128)(2,1)S(1)} %join.3.refs_0_.rest_0_), channel_id=1, source_target_pairs={{0,17},{1,16},{2,19},{3,18},{4,21},{5,20},{6,23},{7,22},{8,25},{9,... | collective-permute-start | bytes 442376 | tf_op jit(solution)/shard_map/ppermute | solution.py:32
  15.0 3.1 %collective-permute-done.22.refs_3_.rest_3_ = bf16[4,144,128]{2,1,0:T(8,128)(2,1)S(1)} collective-permute-done((bf16[4,144,128]{2,1,0:T(8,128)(2,1)S(1)}, bf16[4,144,128]{2,1,0:T(8,128)(2,1)S(1)}, u32[]{:S(2)}, u32[]{:S(2)}) %collective-permute-start.22) | collective-permute-done | bytes 147488 | tf_op jit(solution)/shard_map/ppermute | solution.py:32
  18.1 1.7 %collective-permute-done.21.refs_2_.rest_2_ = bf16[4,144,128]{2,1,0:T(8,128)(2,1)S(1)} collective-permute-done((bf16[4,144,128]{2,1,0:T(8,128)(2,1)S(1)}, bf16[4,144,128]{2,1,0:T(8,128)(2,1)S(1)}, u32[]{:S(2)}, u32[]{:S(2)}) %collective-permute-start.21) | collective-permute-done | bytes 147488 | tf_op jit(solution)/shard_map/ppermute | solution.py:32
  22.1 3.1 %mask.3.amp = bf16[512,4096]{1,0:T(8,128)(2,1)S(1)} custom-call(s32[8,32]{1,0:T(8,128)} %live.1, bf16[512,4096]{1,0:T(8,128)(2,1)} %amp.1), custom_call_target="tpu_custom_call" | custom-call | tf_op jit(solution)/shard_map/mask/pallas_call | solution.py:100
  25.1 1.5 %contract_mine.3.given = f32[512,1024]{1,0:T(8,128)S(1)} custom-call(s32[92]{0:T(128)S(4)} %table.3, bf16[512,4096]{1,0:T(8,128)(2,1)S(1)} %mask.3.amp, bf16[4,144,128]{2,1,0:T(8,128)(2,1)S(1)} %join.3.refs_0_.rest_0_, bf16[4,144,128]{2,1,0:T(8,128)(2,1)S(1)} %collective-permute-done.20.refs_1_.rest_1_, ...), custom_call_target="tpu_custom_call" | custom-call | tf_op jit(solution)/shard_map/contract_mine/pallas_call | solution.py:172
  27.0 1.6 %contract_rest.3 = (bf16[64,1024]{1,0:T(8,128)(2,1)S(1)}, bf16[64,1024]{1,0:T(8,128)(2,1)S(1)}, bf16[64,1024]{1,0:T(8,128)(2,1)S(1)}, bf16[64,1024]{1,0:T(8,128)...) custom-call(s32[92]{0:T(128)S(4)} %table.3, ...), custom_call_target="tpu_custom_call", output_to_operand_aliasing={{7}: (2, {})} | custom-call | tf_op jit(solution)/shard_map/contract_rest/pallas_call | solution.py:204
  30.4 2.3 %collective-permute-start.30 = (bf16[64,1024]{1,0:T(8,128)(2,1)S(1)}, bf16[64,1024]{1,0:T(8,128)(2,1)S(1)}, u32[]{:S(2)}, u32[]{:S(2)}) collective-permute-start(bf16[64,1024]{1,0:T(8,128)(2,1)S(1)} %get-tuple-element.75.rest_0_), channel_id=1, source_target_pairs={{0,4},{1,5},{2,6},{3,7},{4,0},{5,1},{6,2},{7,3},{8,12},{9,13},{10,... | collective-permute-start | bytes 393224 | tf_op jit(solution)/shard_map/ppermute | solution.py:32
  32.6 1.6 %collective-permute-start.29 = (bf16[64,1024]{1,0:T(8,128)(2,1)S(1)}, bf16[64,1024]{1,0:T(8,128)(2,1)S(1)}, u32[]{:S(2)}, u32[]{:S(2)}) collective-permute-start(bf16[64,1024]{1,0:T(8,128)(2,1)S(1)} %get-tuple-element.75.rest_0_), channel_id=1, source_target_pairs={{0,2},{1,3},{2,0},{3,1},{4,6},{5,7},{6,4},{7,5},{8,10},{9,11},{10,... | collective-permute-start | bytes 393224 | tf_op jit(solution)/shard_map/ppermute | solution.py:32
  35.2 1.4 %collective-permute-start.36 = (bf16[64,1024]{1,0:T(8,128)(2,1)S(1)}, bf16[64,1024]{1,0:T(8,128)(2,1)S(1)}, u32[]{:S(2)}, u32[]{:S(2)}) collective-permute-start(bf16[64,1024]{1,0:T(8,128)(2,1)S(1)} %get-tuple-element.79), channel_id=1, source_target_pairs={{0,6},{1,7},{2,4},{3,5},{4,2},{5,3},{6,0},{7,1},{8,14},{9,15},{10,... | collective-permute-start | bytes 393224 | tf_op jit(solution)/shard_map/ppermute | solution.py:32
  36.6 2.2 %collective-permute-done.34.rest_1_ = bf16[64,1024]{1,0:T(8,128)(2,1)S(1)} collective-permute-done((bf16[64,1024]{1,0:T(8,128)(2,1)S(1)}, bf16[64,1024]{1,0:T(8,128)(2,1)S(1)}, u32[]{:S(2)}, u32[]{:S(2)}) %collective-permute-start.34) | collective-permute-done | bytes 131104 | tf_op jit(solution)/shard_map/ppermute | solution.py:32
  39.5 1.9 %collective-permute-start.31 = (bf16[64,1024]{1,0:T(8,128)(2,1)S(1)}, bf16[64,1024]{1,0:T(8,128)(2,1)S(1)}, u32[]{:S(2)}, u32[]{:S(2)}) collective-permute-start(bf16[64,1024]{1,0:T(8,128)(2,1)S(1)} %collective-permute-done.30.rest_2_.rest_6_), channel_id=1, source_target_pairs={{0,2},{1,3},{2,0},{3,1},{4,6},{5,7},{6,4},{7,5},{8,10},{9,11},{10,... | collective-permute-start | bytes 393224 | tf_op jit(solution)/shard_map/ppermute | solution.py:32
  43.4 2.1 %collective-permute-done.35.rest_2_ = bf16[64,1024]{1,0:T(8,128)(2,1)S(1)} collective-permute-done((bf16[64,1024]{1,0:T(8,128)(2,1)S(1)}, bf16[64,1024]{1,0:T(8,128)(2,1)S(1)}, u32[]{:S(2)}, u32[]{:S(2)}) %collective-permute-start.35) | collective-permute-done | bytes 131104 | tf_op jit(solution)/shard_map/ppermute | solution.py:32
  45.5 3.9 %collective-permute-done.36.rest_3_ = bf16[64,1024]{1,0:T(8,128)(2,1)S(1)} collective-permute-done((bf16[64,1024]{1,0:T(8,128)(2,1)S(1)}, bf16[64,1024]{1,0:T(8,128)(2,1)S(1)}, u32[]{:S(2)}, u32[]{:S(2)}) %collective-permute-start.36) | collective-permute-done | bytes 131104 | tf_op jit(solution)/shard_map/ppermute | solution.py:32
  49.4 3.2 %collective-permute-done.37.rest_4_ = bf16[64,1024]{1,0:T(8,128)(2,1)S(1)} collective-permute-done((bf16[64,1024]{1,0:T(8,128)(2,1)S(1)}, bf16[64,1024]{1,0:T(8,128)(2,1)S(1)}, u32[]{:S(2)}, u32[]{:S(2)}) %collective-permute-start.37) | collective-permute-done | bytes 131104 | tf_op jit(solution)/shard_map/ppermute | solution.py:32
  52.6 1.5 %place.4 = bf16[512,1024]{1,0:T(8,128)(2,1)} custom-call(s32[1]{0:T(128)} %crowding.1.crowded, s32[17]{0:T(128)S(4)} %get-tuple-element.131.positions, bf16[64,1024]{1,0:T(8,128)(2,1)S(1)} %collective-permute-done.33.rest_0_, bf16[64,1024]{1,0:T(8,128)(2,1)S(1)} %collective-permute-done.34.rest_1_, ...), custom_call_target="tpu_custom_call", output_to_operand_aliasing={{}: (10, {})} | custom-call | tf_op jit(solution)/shard_map/place/pallas_call | solution.py:397
  54.2 2.2 %collective-permute-start.27 = (bf16[64,1024]{1,0:T(8,128)(2,1)S(1)}, bf16[64,1024]{1,0:T(8,128)(2,1)S(1)}, u32[]{:S(2)}, u32[]{:S(2)}) collective-permute-start(bf16[64,1024]{1,0:T(8,128)(2,1)S(1)} %get-tuple-element.72), channel_id=1, source_target_pairs={{0,4},{1,5},{2,6},{3,7},{4,0},{5,1},{6,2},{7,3},{8,12},{9,13},{10,... | collective-permute-start | bytes 393224 | tf_op jit(solution)/shard_map/ppermute | solution.py:32
  56.5 1.2 %collective-permute-start.28 = (bf16[64,1024]{1,0:T(8,128)(2,1)S(1)}, bf16[64,1024]{1,0:T(8,128)(2,1)S(1)}, u32[]{:S(2)}, u32[]{:S(2)}) collective-permute-start(bf16[64,1024]{1,0:T(8,128)(2,1)S(1)} %get-tuple-element.73), channel_id=1, source_target_pairs={{0,5},{1,4},{2,7},{3,6},{4,1},{5,0},{6,3},{7,2},{8,13},{9,12},{10,... | collective-permute-start | bytes 393224 | tf_op jit(solution)/shard_map/ppermute | solution.py:32
  57.7 1.1 %collective-permute-start.32 = (bf16[64,1024]{1,0:T(8,128)(2,1)S(1)}, bf16[64,1024]{1,0:T(8,128)(2,1)S(1)}, u32[]{:S(2)}, u32[]{:S(2)}) collective-permute-start(bf16[64,1024]{1,0:T(8,128)(2,1)S(1)} %choose.1), channel_id=1, source_target_pairs={{0,1},{1,0},{2,3},{3,2},{4,5},{5,4},{6,7},{7,6},{8,9},{9,8},{10,11... | collective-permute-start | bytes 393224 | tf_op jit(solution)/shard_map/ppermute | solution.py:32
  58.8 6.9 %collective-permute-done.27.rest_0_ = bf16[64,1024]{1,0:T(8,128)(2,1)S(1)} collective-permute-done((bf16[64,1024]{1,0:T(8,128)(2,1)S(1)}, bf16[64,1024]{1,0:T(8,128)(2,1)S(1)}, u32[]{:S(2)}, u32[]{:S(2)}) %collective-permute-start.27) | collective-permute-done | bytes 131104 | tf_op jit(solution)/shard_map/ppermute | solution.py:32
  65.7 2.3 %collective-permute-done.28.rest_1_ = bf16[64,1024]{1,0:T(8,128)(2,1)S(1)} collective-permute-done((bf16[64,1024]{1,0:T(8,128)(2,1)S(1)}, bf16[64,1024]{1,0:T(8,128)(2,1)S(1)}, u32[]{:S(2)}, u32[]{:S(2)}) %collective-permute-start.28) | collective-permute-done | bytes 131104 | tf_op jit(solution)/shard_map/ppermute | solution.py:32
  68.0 1.4 %place.5 = bf16[512,1024]{1,0:T(8,128)(2,1)} custom-call(s32[1]{0:T(128)} %crowding.1.crowded, s32[17]{0:T(128)S(4)} %get-tuple-element.131.positions, bf16[64,1024]{1,0:T(8,128)(2,1)S(1)} %collective-permute-done.27.rest_0_, bf16[64,1024]{1,0:T(8,128)(2,1)S(1)} %collective-permute-done.28.rest_1_, ...), custom_call_target="tpu_custom_call", output_to_operand_aliasing={{}: (5, {})} | custom-call | tf_op jit(solution)/shard_map/place/pallas_call | solution.py:397
  (40 shorter events, 10.4 us)
Async XLA Ops:
  1.5 7.0 %collective-permute-start.19 = (bf16[1,144,128]{2,1,0:T(8,128)(2,1)S(1)}, bf16[1,144,128]{2,1,0:T(8,128)(2,1)S(1)}, u32[]{:S(2)}, u32[]{:S(2)}) collective-permute-start(bf16[1,144,128]{2,1,0:T(8,128)(2,1)S(1)} %pad_maximum_fusion.1.refs_0_), channel_id=1, source_target_pairs={{0,6},{1,7},{2,4},{3,5},{4,2},{5,3},{6,0},{7,1},{8,14},{9,15},{10,... | collective-permute-start | bytes 110600 | tf_op jit(solution)/shard_map/ppermute | solution.py:32
  6.5 4.9 %collective-permute-start.18 = (bf16[1,144,128]{2,1,0:T(8,128)(2,1)S(1)}, bf16[1,144,128]{2,1,0:T(8,128)(2,1)S(1)}, u32[]{:S(2)}, u32[]{:S(2)}) collective-permute-start(bf16[1,144,128]{2,1,0:T(8,128)(2,1)S(1)} %pad_maximum_fusion.1.refs_0_), channel_id=1, source_target_pairs={{0,4},{1,5},{2,6},{3,7},{4,0},{5,1},{6,2},{7,3},{8,12},{9,13},{10,... | collective-permute-start | bytes 110600 | tf_op jit(solution)/shard_map/ppermute | solution.py:32
  6.5 4.9 %collective-permute-start.17 = (bf16[1,144,128]{2,1,0:T(8,128)(2,1)S(1)}, bf16[1,144,128]{2,1,0:T(8,128)(2,1)S(1)}, u32[]{:S(2)}, u32[]{:S(2)}) collective-permute-start(bf16[1,144,128]{2,1,0:T(8,128)(2,1)S(1)} %pad_maximum_fusion.1.refs_0_), channel_id=1, source_target_pairs={{0,2},{1,3},{2,0},{3,1},{4,6},{5,7},{6,4},{7,5},{8,10},{9,11},{10,... | collective-permute-start | bytes 110600 | tf_op jit(solution)/shard_map/ppermute | solution.py:32
  11.4 6.7 %collective-permute-start.22 = (bf16[4,144,128]{2,1,0:T(8,128)(2,1)S(1)}, bf16[4,144,128]{2,1,0:T(8,128)(2,1)S(1)}, u32[]{:S(2)}, u32[]{:S(2)}) collective-permute-start(bf16[4,144,128]{2,1,0:T(8,128)(2,1)S(1)} %join.3.refs_0_.rest_0_), channel_id=1, source_target_pairs={{0,17},{1,16},{2,19},{3,18},{4,21},{5,20},{6,23},{7,22},{8,25},{9,... | collective-permute-start | bytes 442376 | tf_op jit(solution)/shard_map/ppermute | solution.py:32
  13.9 5.9 %collective-permute-start.21 = (bf16[4,144,128]{2,1,0:T(8,128)(2,1)S(1)}, bf16[4,144,128]{2,1,0:T(8,128)(2,1)S(1)}, u32[]{:S(2)}, u32[]{:S(2)}) collective-permute-start(bf16[4,144,128]{2,1,0:T(8,128)(2,1)S(1)} %join.3.refs_0_.rest_0_), channel_id=1, source_target_pairs={{0,16},{1,17},{2,18},{3,19},{4,20},{5,21},{6,22},{7,23},{8,24},{9,... | collective-permute-start | bytes 442376 | tf_op jit(solution)/shard_map/ppermute | solution.py:32
  14.5 5.3 %collective-permute-start.20 = (bf16[4,144,128]{2,1,0:T(8,128)(2,1)S(1)}, bf16[4,144,128]{2,1,0:T(8,128)(2,1)S(1)}, u32[]{:S(2)}, u32[]{:S(2)}) collective-permute-start(bf16[4,144,128]{2,1,0:T(8,128)(2,1)S(1)} %join.3.refs_0_.rest_0_), channel_id=1, source_target_pairs={{0,1},{1,0},{2,3},{3,2},{4,5},{5,4},{6,7},{7,6},{8,9},{9,8},{10,11... | collective-permute-start | bytes 442376 | tf_op jit(solution)/shard_map/ppermute | solution.py:32
  15.0 11.7 %collective-permute-start.23 = (bf16[4,144,128]{2,1,0:T(8,128)(2,1)S(1)}, bf16[4,144,128]{2,1,0:T(8,128)(2,1)S(1)}, u32[]{:S(2)}, u32[]{:S(2)}) collective-permute-start(bf16[4,144,128]{2,1,0:T(8,128)(2,1)S(1)} %join.3.refs_0_.rest_0_), channel_id=1, source_target_pairs={{0,8},{1,9},{2,10},{3,11},{4,12},{5,13},{6,14},{7,15},{8,0},{9,1},... | collective-permute-start | bytes 442376 | tf_op jit(solution)/shard_map/ppermute | solution.py:32
  18.1 8.6 %collective-permute-start.26 = (bf16[4,144,128]{2,1,0:T(8,128)(2,1)S(1)}, bf16[4,144,128]{2,1,0:T(8,128)(2,1)S(1)}, u32[]{:S(2)}, u32[]{:S(2)}) collective-permute-start(bf16[4,144,128]{2,1,0:T(8,128)(2,1)S(1)} %collective-permute-done.22.refs_3_.rest_3_), channel_id=1, source_target_pairs={{0,8},{1,9},{2,10},{3,11},{4,12},{5,13},{6,14},{7,15},{8,0},{9,1},... | collective-permute-start | bytes 442376 | tf_op jit(solution)/shard_map/ppermute | solution.py:32
  19.8 6.9 %collective-permute-start.25 = (bf16[4,144,128]{2,1,0:T(8,128)(2,1)S(1)}, bf16[4,144,128]{2,1,0:T(8,128)(2,1)S(1)}, u32[]{:S(2)}, u32[]{:S(2)}) collective-permute-start(bf16[4,144,128]{2,1,0:T(8,128)(2,1)S(1)} %collective-permute-done.21.refs_2_.rest_2_), channel_id=1, source_target_pairs={{0,8},{1,9},{2,10},{3,11},{4,12},{5,13},{6,14},{7,15},{8,0},{9,1},... | collective-permute-start | bytes 442376 | tf_op jit(solution)/shard_map/ppermute | solution.py:32
  19.8 6.9 %collective-permute-start.24 = (bf16[4,144,128]{2,1,0:T(8,128)(2,1)S(1)}, bf16[4,144,128]{2,1,0:T(8,128)(2,1)S(1)}, u32[]{:S(2)}, u32[]{:S(2)}) collective-permute-start(bf16[4,144,128]{2,1,0:T(8,128)(2,1)S(1)} %collective-permute-done.20.refs_1_.rest_1_), channel_id=1, source_target_pairs={{0,8},{1,9},{2,10},{3,11},{4,12},{5,13},{6,14},{7,15},{8,0},{9,1},... | collective-permute-start | bytes 442376 | tf_op jit(solution)/shard_map/ppermute | solution.py:32
  28.7 6.5 %collective-permute-start.33 = (bf16[64,1024]{1,0:T(8,128)(2,1)S(1)}, bf16[64,1024]{1,0:T(8,128)(2,1)S(1)}, u32[]{:S(2)}, u32[]{:S(2)}) collective-permute-start(bf16[64,1024]{1,0:T(8,128)(2,1)S(1)} %get-tuple-element.76), channel_id=1, source_target_pairs={{0,1},{1,0},{2,3},{3,2},{4,5},{5,4},{6,7},{7,6},{8,9},{9,8},{10,11... | collective-permute-start | bytes 393224 | tf_op jit(solution)/shard_map/ppermute | solution.py:32
  29.6 9.2 %collective-permute-start.34 = (bf16[64,1024]{1,0:T(8,128)(2,1)S(1)}, bf16[64,1024]{1,0:T(8,128)(2,1)S(1)}, u32[]{:S(2)}, u32[]{:S(2)}) collective-permute-start(bf16[64,1024]{1,0:T(8,128)(2,1)S(1)} %get-tuple-element.77), channel_id=1, source_target_pairs={{0,2},{1,3},{2,0},{3,1},{4,6},{5,7},{6,4},{7,5},{8,10},{9,11},{10,... | collective-permute-start | bytes 393224 | tf_op jit(solution)/shard_map/ppermute | solution.py:32
  30.4 9.1 %collective-permute-start.30 = (bf16[64,1024]{1,0:T(8,128)(2,1)S(1)}, bf16[64,1024]{1,0:T(8,128)(2,1)S(1)}, u32[]{:S(2)}, u32[]{:S(2)}) collective-permute-start(bf16[64,1024]{1,0:T(8,128)(2,1)S(1)} %get-tuple-element.75.rest_0_), channel_id=1, source_target_pairs={{0,4},{1,5},{2,6},{3,7},{4,0},{5,1},{6,2},{7,3},{8,12},{9,13},{10,... | collective-permute-start | bytes 393224 | tf_op jit(solution)/shard_map/ppermute | solution.py:32
  32.6 20.0 %collective-permute-start.29 = (bf16[64,1024]{1,0:T(8,128)(2,1)S(1)}, bf16[64,1024]{1,0:T(8,128)(2,1)S(1)}, u32[]{:S(2)}, u32[]{:S(2)}) collective-permute-start(bf16[64,1024]{1,0:T(8,128)(2,1)S(1)} %get-tuple-element.75.rest_0_), channel_id=1, source_target_pairs={{0,2},{1,3},{2,0},{3,1},{4,6},{5,7},{6,4},{7,5},{8,10},{9,11},{10,... | collective-permute-start | bytes 393224 | tf_op jit(solution)/shard_map/ppermute | solution.py:32
  34.2 11.3 %collective-permute-start.35 = (bf16[64,1024]{1,0:T(8,128)(2,1)S(1)}, bf16[64,1024]{1,0:T(8,128)(2,1)S(1)}, u32[]{:S(2)}, u32[]{:S(2)}) collective-permute-start(bf16[64,1024]{1,0:T(8,128)(2,1)S(1)} %get-tuple-element.78), channel_id=1, source_target_pairs={{0,3},{1,2},{2,1},{3,0},{4,7},{5,6},{6,5},{7,4},{8,11},{9,10},{10,... | collective-permute-start | bytes 393224 | tf_op jit(solution)/shard_map/ppermute | solution.py:32
  35.2 14.2 %collective-permute-start.36 = (bf16[64,1024]{1,0:T(8,128)(2,1)S(1)}, bf16[64,1024]{1,0:T(8,128)(2,1)S(1)}, u32[]{:S(2)}, u32[]{:S(2)}) collective-permute-start(bf16[64,1024]{1,0:T(8,128)(2,1)S(1)} %get-tuple-element.79), channel_id=1, source_target_pairs={{0,6},{1,7},{2,4},{3,5},{4,2},{5,3},{6,0},{7,1},{8,14},{9,15},{10,... | collective-permute-start | bytes 393224 | tf_op jit(solution)/shard_map/ppermute | solution.py:32
  38.8 13.8 %collective-permute-start.37 = (bf16[64,1024]{1,0:T(8,128)(2,1)S(1)}, bf16[64,1024]{1,0:T(8,128)(2,1)S(1)}, u32[]{:S(2)}, u32[]{:S(2)}) collective-permute-start(bf16[64,1024]{1,0:T(8,128)(2,1)S(1)} %get-tuple-element.80), channel_id=1, source_target_pairs={{0,7},{1,6},{2,5},{3,4},{4,3},{5,2},{6,1},{7,0},{8,15},{9,14},{10,... | collective-permute-start | bytes 393224 | tf_op jit(solution)/shard_map/ppermute | solution.py:32
  39.5 13.2 %collective-permute-start.31 = (bf16[64,1024]{1,0:T(8,128)(2,1)S(1)}, bf16[64,1024]{1,0:T(8,128)(2,1)S(1)}, u32[]{:S(2)}, u32[]{:S(2)}) collective-permute-start(bf16[64,1024]{1,0:T(8,128)(2,1)S(1)} %collective-permute-done.30.rest_2_.rest_6_), channel_id=1, source_target_pairs={{0,2},{1,3},{2,0},{3,1},{4,6},{5,7},{6,4},{7,5},{8,10},{9,11},{10,... | collective-permute-start | bytes 393224 | tf_op jit(solution)/shard_map/ppermute | solution.py:32
  41.9 12.3 %copy-start = (bf16[1,128,128]{2,1,0:T(8,128)(2,1)S(1)}, bf16[1,128,128]{2,1,0:T(8,128)(2,1)}, u32[]{:S(2)}) copy-start(bf16[1,128,128]{2,1,0:T(8,128)(2,1)} %param.11) | copy-start | bytes 98308
  41.9 12.3 %copy-start.1 = (s32[8,32]{1,0:T(8,128)S(1)}, s32[8,32]{1,0:T(8,128)}, u32[]{:S(2)}) copy-start(s32[8,32]{1,0:T(8,128)} %live.1) | copy-start | bytes 3076
  41.9 12.3 %copy-start.2 = (s32[8]{0:T(128)S(1)}, s32[8]{0:T(128)}, u32[]{:S(2)}) copy-start(s32[8]{0:T(128)} %destination.1) | copy-start | bytes 100
  54.2 11.5 %collective-permute-start.27 = (bf16[64,1024]{1,0:T(8,128)(2,1)S(1)}, bf16[64,1024]{1,0:T(8,128)(2,1)S(1)}, u32[]{:S(2)}, u32[]{:S(2)}) collective-permute-start(bf16[64,1024]{1,0:T(8,128)(2,1)S(1)} %get-tuple-element.72), channel_id=1, source_target_pairs={{0,4},{1,5},{2,6},{3,7},{4,0},{5,1},{6,2},{7,3},{8,12},{9,13},{10,... | collective-permute-start | bytes 393224 | tf_op jit(solution)/shard_map/ppermute | solution.py:32
  56.5 11.5 %collective-permute-start.28 = (bf16[64,1024]{1,0:T(8,128)(2,1)S(1)}, bf16[64,1024]{1,0:T(8,128)(2,1)S(1)}, u32[]{:S(2)}, u32[]{:S(2)}) collective-permute-start(bf16[64,1024]{1,0:T(8,128)(2,1)S(1)} %get-tuple-element.73), channel_id=1, source_target_pairs={{0,5},{1,4},{2,7},{3,6},{4,1},{5,0},{6,3},{7,2},{8,13},{9,12},{10,... | collective-permute-start | bytes 393224 | tf_op jit(solution)/shard_map/ppermute | solution.py:32
  57.7 10.3 %collective-permute-start.32 = (bf16[64,1024]{1,0:T(8,128)(2,1)S(1)}, bf16[64,1024]{1,0:T(8,128)(2,1)S(1)}, u32[]{:S(2)}, u32[]{:S(2)}) collective-permute-start(bf16[64,1024]{1,0:T(8,128)(2,1)S(1)} %choose.1), channel_id=1, source_target_pairs={{0,1},{1,0},{2,3},{3,2},{4,5},{5,4},{6,7},{7,6},{8,9},{9,8},{10,11... | collective-permute-start | bytes 393224 | tf_op jit(solution)/shard_map/ppermute | solution.py:32

commit v2 on v1

--- a/solution.py
+++ b/solution.py
@@ -9,7 +9,6 @@
 
 
 AT = 8
-META = 16
 
 
 GRANT = pltpu.CompilerParams(vmem_limit_bytes=40 * 1024 * 1024)
@@ -18,8 +17,9 @@
 SMEM = pl.BlockSpec(memory_space=pltpu.SMEM)
 ANY = pl.BlockSpec(memory_space=pl.ANY)
 HBM = pl.BlockSpec(memory_space=pltpu.HBM)
+LAST = (None, None)
 NONE = 1 << 20
-LAST = (None, None)
+META = 16
 
 
 def swap(value, mask, sizes):
@@ -36,23 +36,55 @@
     return pltpu.with_memory_space_constraint(value, pltpu.VMEM)
 
 
+def block_kernel(cols, destination, integrals, out, rows):
+    held, width, _ = integrals.shape
+    tiles = destination.shape[1]
+    rows[...] = jnp.full(rows.shape, -1.0, rows.dtype)
+    owner, spot = split(destination[...], tiles)
+    rows[0:1, :tiles] = split(owner, cols)[1].astype(rows.dtype)
+    rows[1:2, :tiles] = spot.astype(rows.dtype)
+    for t in range(held):
+        out[t, :width, :] = integrals[t]
+        out[t, width:, :] = rows[...].astype(out.dtype)
+
+
+def make_block(destination, integrals, cols):
+    held, width, _ = integrals.shape
+    return pl.pallas_call(
+        functools.partial(block_kernel, cols),
+        out_shape=pltpu.VMEM((held, width + META, width), integrals.dtype),
+        in_specs=[VMEM, VMEM],
+        out_specs=VMEM,
+        scratch_shapes=[pltpu.VMEM((META, width), jnp.float32)],
+        compiler_params=SMALL,
+        name="block",
+    )(destination[None], integrals)
+
+
 def join_kernel(*refs):
-    out = refs[-1]
-    size = refs[0].shape[0]
-    for n, ref in enumerate(refs[:-1]):
-        out[n * size : (n + 1) * size] = ref[...]
+    pieces, out, rows = refs[:4], refs[4], refs[5]
+    held, _, width = pieces[0].shape
+    rows[...] = jnp.full(rows.shape, -1.0, rows.dtype)
+    for n, piece in enumerate(pieces):
+        for t in range(held):
+            start = (n * held + t) * width
+            out[start : start + width, :] = piece[t, :width, :]
+        told = piece[0, width:, :].astype(rows.dtype)
+        rows[2 * n : 2 * n + 2, :] = told[0:2]
+    out[4 * held * width :, :] = rows[...].astype(out.dtype)
 
 
 def join(pieces):
-    shape = pieces[0].shape
+    held, _, width = pieces[0].shape
     return pl.pallas_call(
         join_kernel,
-        out_shape=pltpu.VMEM((len(pieces) * shape[0], *shape[1:]), pieces[0].dtype),
-        in_specs=[VMEM] * len(pieces),
+        out_shape=pltpu.VMEM((4 * held * width + META, width), pieces[0].dtype),
+        in_specs=[VMEM] * 4,
         out_specs=VMEM,
+        scratch_shapes=[pltpu.VMEM((META, width), jnp.float32)],
         compiler_params=SMALL,
         name="join",
-    )(*[local(piece) for piece in pieces])
+    )(*[local(x) for x in pieces])
 
 
 def gather_all(block, sizes):
@@ -66,10 +98,11 @@
     mine, other = {0: line}, {}
     for n in reversed(range(1, len(near))):
         mine[n] = swap(line, near[n], sizes)
-    for n in range(len(near)):
+    for n in mine:
         other[n] = swap(mine[n], (1, 0), sizes)
-    count = range(len(near))
-    return [local(mine[n]) for n in count], [local(other[n]) for n in count]
+    gathered = {(0, n): local(mine[n]) for n in mine}
+    gathered.update({(1, n): local(other[n]) for n in other})
+    return gathered, list(mine)
 
 
 def gather_mask(q, half, cols):
@@ -108,48 +141,48 @@
     )(live, pltpu.with_memory_space_constraint(amp, pltpu.HBM))
 
 
-def add_tiles(places, total, refs, half, held_tiles, cols, rows):
+def add_tiles(places, total, parts, refs, held_tiles, cols, rows):
     my_row, my_col = lax.axis_index("row"), lax.axis_index("col")
     base, step = places_at(cols), cols // 4
 
-    def add(ref, line, q):
-        width = ref.shape[2]
+    def add(ref, half, line, q):
+        width = ref.shape[1]
         far = q // held_tiles
         row_mask, col_mask = 2 * (line // step) + half, line % step + far * step
         entry = ((my_row ^ row_mask) * cols + (my_col ^ col_mask)) * held_tiles + q % held_tiles
         k, a = places[base + 2 * entry], places[base + 2 * entry + 1]
         inner = pl.ds(pl.multiple_of(k * width, width), width)
         outer = pl.ds(pl.multiple_of(a * width, width), width)
-        right = ref[q, pl.ds(0, width), :]
-        total[:, outer] += jnp.dot(rows(inner), right, preferred_element_type=jnp.float32)
-
-    for line, ref in enumerate(refs):
-        for q in range(ref.shape[0]):
-            add(ref, line, q)
-
-
-def contract_mine_kernel(held_tiles, cols, table, amp, *rest):
-    mine, total = rest[:-1], rest[-1]
-    total[...] = jnp.zeros_like(total)
-    add_tiles(table, total, mine, 0, held_tiles, cols, lambda inner: amp[:, inner])
-
-
-def contract_one_kernel(slot, pair_rows, held_tiles, cols, table, amp, given, *rest):
-    other, (out, _, one) = rest[:-3], rest[-3:]
+        total[:, outer] += jnp.dot(rows(inner), ref[q * width : (q + 1) * width, :], preferred_element_type=jnp.float32)
+
+    for (half, line), ref in zip(parts, refs):
+        for q in range(4 * held_tiles):
+            add(ref, half, line, q)
+
+
+def contract_all_kernel(parts, fresh, held_tiles, cols, table, amp, *rest):
+    refs, total = rest[: len(parts)], rest[-1]
+    if fresh:
+        total[...] = jnp.zeros_like(total)
+    add_tiles(table, total, parts, refs, held_tiles, cols, lambda inner: amp[:, inner])
+
+
+def contract_one_kernel(slot, parts, pair_rows, held_tiles, cols, table, amp, given, *rest):
+    refs, (out, _, one) = rest[:-3], rest[-3:]
     picked = pl.ds(pl.multiple_of(table[slot] * pair_rows, pair_rows), pair_rows)
     one[...] = given[picked, :]
-    add_tiles(table, one, other, 1, held_tiles, cols, lambda inner: amp[picked, inner])
+    add_tiles(table, one, parts, refs, held_tiles, cols, lambda inner: amp[picked, inner])
     out[...] = one[...].astype(out.dtype)
 
 
 def contract_rest_kernel(slots, own, parts, pair_rows, held_tiles, cols, table, amp, given, *rest):
-    other, rest = rest[:parts], rest[parts:]
+    refs, rest = rest[: len(parts)], rest[len(parts) :]
     outs = rest[: len(slots)]
     if own:
         total, ladder, kept, sems = rest[len(slots) :]
     else:
         (total,) = rest[len(slots) :]
-    add_tiles(table, total, other, 1, held_tiles, cols, lambda inner: amp[:, inner])
+    add_tiles(table, total, parts, refs, held_tiles, cols, lambda inner: amp[:, inner])
 
     def product(slot):
         start = pl.multiple_of(table[slot] * pair_rows, pair_rows)
@@ -168,32 +201,38 @@
         pl.when(there)(copy.wait)
 
 
-def contract_mine(table, amp, mine, sizes):
-    return pl.pallas_call(
-        functools.partial(contract_mine_kernel, *sizes[1:]),
-        out_shape=pltpu.VMEM((amp.shape[0], AT * mine[0].shape[2]), jnp.float32),
-        in_specs=[SMEM, VMEM] + [VMEM] * len(mine),
+def contract_all(table, amp, gathered, parts, sizes, total=None):
+    refs = [gathered[part] for part in parts]
+    shape = (amp.shape[0], AT * refs[0].shape[1])
+    given = [] if total is None else [total]
+    return pl.pallas_call(
+        functools.partial(contract_all_kernel, parts, total is None, *sizes[1:]),
+        out_shape=pltpu.VMEM(shape, jnp.float32),
+        in_specs=[SMEM] + [VMEM] * (1 + len(refs) + len(given)),
         out_specs=VMEM,
+        input_output_aliases={2 + len(refs): 0} if given else {},
         compiler_params=GRANT,
-        name="contract_mine",
-    )(table, amp, *mine)
-
-
-def contract_one(slot, table, amp, other, total, sizes):
+        name="contract_all",
+    )(table, amp, *refs, *given)
+
+
+def contract_one(slot, table, amp, gathered, parts, total, sizes):
+    refs = [gathered[part] for part in parts]
     shape = (sizes[0], total.shape[1])
     return pl.pallas_call(
-        functools.partial(contract_one_kernel, slot, *sizes),
+        functools.partial(contract_one_kernel, slot, parts, *sizes),
         out_shape=[pltpu.VMEM(shape, amp.dtype), pltpu.VMEM(total.shape, total.dtype)],
-        in_specs=[SMEM, VMEM, VMEM] + [VMEM] * len(other),
+        in_specs=[SMEM] + [VMEM] * (2 + len(refs)),
         out_specs=[VMEM, VMEM],
         scratch_shapes=[pltpu.VMEM(shape, jnp.float32)],
         input_output_aliases={2: 1},
         compiler_params=GRANT,
         name="contract_one",
-    )(table, amp, total, *other)
-
-
-def contract_rest(slots, own, table, amp, other, total, sizes):
+    )(table, amp, total, *refs)
+
+
+def contract_rest(slots, own, table, amp, gathered, parts, total, sizes):
+    refs = [gathered[part] for part in parts]
     shape = (sizes[0], total.shape[1])
     out_shape = [pltpu.VMEM(shape, amp.dtype)] * len(slots)
     out_shape.append(pltpu.VMEM(total.shape, total.dtype))
@@ -202,15 +241,15 @@
         out_shape.append(pltpu.HBM(total.shape, amp.dtype))
         scratch = [pltpu.VMEM((len(own), *shape), amp.dtype), pltpu.SemaphoreType.DMA((len(own),))]
     return pl.pallas_call(
-        functools.partial(contract_rest_kernel, slots, own, len(other), *sizes),
+        functools.partial(contract_rest_kernel, slots, own, parts, *sizes),
         out_shape=out_shape,
-        in_specs=[SMEM, VMEM, VMEM] + [VMEM] * len(other),
+        in_specs=[SMEM] + [VMEM] * (2 + len(refs)),
         out_specs=[VMEM] * (len(slots) + 1) + [HBM] * (1 if own else 0),
         scratch_shapes=scratch,
         input_output_aliases={2: len(slots)},
         compiler_params=GRANT,
         name="contract_rest",
-    )(table, amp, total, *other)
+    )(table, amp, total, *refs)
 
 
 def places_at(cols):
@@ -226,8 +265,8 @@
     table[cols + 2] = -1
     table[cols + 3] = -1
     for s in range(count):
-        mask = destination[s] // count % cols ^ my_col
-        spot = destination[s] % count
+        owner, spot = split(destination[s], count)
+        mask = split(owner, cols)[1] ^ my_col
         seen = table[seen_at + mask]
         table[seen_at + mask] = seen + 1
 
@@ -251,13 +290,13 @@
         def _(s=s):
             table[cols + 1] = s
 
-    for n in range(integrals.shape[0]):
-        table[base + 2 * n] = integrals[n, 0]
-        table[base + 2 * n + 1] = integrals[n, 1]
+    for n in range(integrals.shape[1]):
+        table[base + 2 * n] = integrals[0, n]
+        table[base + 2 * n + 1] = integrals[1, n]
 
 
 def make_table(destination, integrals, cols):
-    size = places_at(cols) + 2 * integrals.shape[0]
+    size = places_at(cols) + 2 * integrals.shape[1]
     return pl.pallas_call(
         functools.partial(table_kernel, cols),
         out_shape=pltpu.SMEM((size,), jnp.int32),
@@ -268,15 +307,21 @@
     )(destination, integrals)
 
 
-def destinations(block, width):
-    told = block[pl.ds(width, META), :].astype(jnp.float32)
-    return told[0:1], told[1:2]
-
-
-def arrivals_kernel(slots, width, *refs):
+def split(value, size):
+    if size & (size - 1):
+        return lax.div(value, size), lax.rem(value, size)
+    return lax.shift_right_logical(value, size.bit_length() - 1), value & (size - 1)
+
+
+def destinations(ref, far):
+    told = ref[pl.ds(ref.shape[0] - META, META), :].astype(jnp.float32)
+    return told[2 * far : 2 * far + 1], told[2 * far + 1 : 2 * far + 2]
+
+
+def arrivals_kernel(slots, *refs):
     my_col = lax.axis_index("col")
     mine, (positions, onward) = refs[:-2], refs[-2:]
-    told = [destinations(mine[n].at[q], width) for n, q in slots]
+    told = [destinations(mine[n], far) for n, far in slots]
     column = jnp.concatenate([t[0] for t in told], axis=0).astype(jnp.int32)
     spot = jnp.concatenate([t[1] for t in told], axis=0).astype(jnp.int32)
     lane = lax.broadcasted_iota(jnp.int32, column.shape, 1)
@@ -307,9 +352,9 @@
     positions[2 * len(slots)] = odd
 
 
-def arrivals(mine, slots, width):
-    return pl.pallas_call(
-        functools.partial(arrivals_kernel, slots, width),
+def arrivals(mine, slots):
+    return pl.pallas_call(
+        functools.partial(arrivals_kernel, slots),
         out_shape=[
             pltpu.SMEM((2 * len(slots) + 1,), jnp.int32),
             pltpu.SMEM((1,), jnp.int32),
@@ -321,13 +366,13 @@
     )(*mine)
 
 
-def crowding_kernel(groups, width, *refs):
+def crowding_kernel(groups, *refs):
     my_col = lax.axis_index("col")
     refs, crowded = refs[:-1], refs[-1]
     worst = jnp.int32(0)
     for slots in groups:
-        blocks = [refs[n].at[q] for n, q in slots]
-        column = jnp.concatenate([destinations(b, width)[0] for b in blocks], axis=0)
+        column = [destinations(refs[n], far)[0] for n, far in slots]
+        column = jnp.concatenate(column, axis=0)
         column = column.astype(jnp.int32)
         lane = lax.broadcasted_iota(jnp.int32, column.shape, 1)
         owner = lax.broadcasted_iota(jnp.int32, column.shape, 0) ^ my_col
@@ -342,9 +387,9 @@
     crowded[0] = worst
 
 
-def crowding(blocks, groups, width):
-    return pl.pallas_call(
-        functools.partial(crowding_kernel, groups, width),
+def crowding(blocks, groups):
+    return pl.pallas_call(
+        functools.partial(crowding_kernel, groups),
         out_shape=jax.ShapeDtypeStruct((1,), jnp.int32),
         in_specs=[VMEM] * len(blocks),
         out_specs=SMEM,
@@ -373,52 +418,37 @@
     )(onward, *choices)
 
 
-def place_kernel(places, guarded, crowded, positions, *rest):
+def place_kernel(places, positions, *rest):
     sources = rest[: len(places)]
     out, left = rest[-2:]
     rows = sources[0].shape[0]
 
-    def there(n):
-        here = positions[places[n]] >= 0
-        return jnp.logical_and(here, crowded[0] <= 1) if places[n] == guarded else here
-
     def store(n):
         start = pl.multiple_of(jnp.maximum(positions[places[n]], 0) * rows, rows)
         return pltpu.make_async_copy(sources[n], out.at[pl.ds(start, rows), :], left.at[n])
 
     for n in range(len(places)):
-        pl.when(there(n))(lambda n=n: store(n).start())
+        pl.when(positions[places[n]] >= 0)(lambda n=n: store(n).start())
     for n in range(len(places)):
-        pl.when(there(n))(lambda n=n: store(n).wait())
-
-
-def place(places, crowded, positions, sources, ladder, guarded=None):
+        pl.when(positions[places[n]] >= 0)(lambda n=n: store(n).wait())
+
+
+def place(places, positions, sources, ladder):
     count = len(sources)
     return pl.pallas_call(
-        functools.partial(place_kernel, places, guarded),
+        functools.partial(place_kernel, places),
         out_shape=pltpu.HBM(ladder.shape, ladder.dtype),
-        in_specs=[SMEM, SMEM] + [VMEM] * count + [HBM],
+        in_specs=[SMEM] + [VMEM] * count + [HBM],
         out_specs=HBM,
         scratch_shapes=[pltpu.SemaphoreType.DMA((count,))],
-        input_output_aliases={2 + count: 0},
+        input_output_aliases={1 + count: 0},
         compiler_params=SMALL,
         name="place",
-    )(crowded, positions, *sources, ladder)
+    )(positions, *sources, ladder)
 
 
 def shards(sizes, *arrays):
     return step(sizes, *arrays)
-
-
-def make_block(destination, integral_tiles, cols):
-    tile_count = destination.shape[0]
-    held_tiles, width, _ = integral_tiles.shape
-    to_col = destination // tile_count % cols
-    to_place = destination % tile_count
-    meta = jnp.stack([to_col, to_place]).astype(integral_tiles.dtype)
-    meta = jnp.pad(meta, ((0, META - 2), (0, width - tile_count)), constant_values=-1)
-    meta = jnp.broadcast_to(meta[None], (held_tiles, META, width))
-    return jnp.concatenate([integral_tiles, meta], axis=1)
 
 
 def hops(cols):
@@ -441,22 +471,26 @@
     tile_count = destination.shape[0]
     pair_rows = amplitudes.shape[0] // tile_count
     held_tiles, width, _ = integral_tiles.shape
-    block = make_block(destination, integral_tiles, cols)
     masked = mask_amplitudes(live_tiles, amplitudes, pair_rows, width)
-    mine, other = gather_all(block, sizes)
-    table = make_table(destination, integral_list, cols)
+    gathered, came = gather_all(make_block(destination, integral_tiles, cols), sizes)
+    table = make_table(destination, integral_list.T, cols)
     shape = (pair_rows, held_tiles, cols)
-    total = contract_mine(table, masked, mine, shape)
-    extra_tile, total = contract_one(cols + 1, table, masked, other, total, shape)
+    soon, late = came[: len(came) // 2], came[len(came) // 2 :]
+    total = contract_all(table, masked, gathered, [(0, n) for n in soon], shape)
+    parts = [(0, n) for n in late] + [(1, n) for n in soon]
+    total = contract_all(table, masked, gathered, parts, shape, total)
+    parts = [(1, n) for n in late]
+    extra_tile, total = contract_one(cols + 1, table, masked, gathered, parts, total, shape)
     slots = list(range(1, cols))
     own = [(0, cols + 2), (cols, cols + 3)]
-    *outs, _, ladder = contract_rest(slots, own, table, masked, other, total, shape)
+    *outs, _, ladder = contract_rest(slots, own, table, masked, gathered, parts, total, shape)
 
     held = [gather_mask(q, half, cols) for half in (0, 1) for q in range(rows * cols // 2)]
-    index = {m: (n // 4, n % 4 * held_tiles) for n, m in enumerate(held)}
+    index = {m: (n // 4, n % 4) for n, m in enumerate(held)}
     groups = [[index[(r, c)] for c in range(cols)] for r in range(rows)]
-    positions, onward = arrivals(mine, groups[0], width)
-    crowded = crowding(mine + other, groups, width)
+    order = sorted(came)
+    positions, onward = arrivals([gathered[0, n] for n in order], groups[0])
+    crowded = crowding([gathered[h, n] for h in (0, 1) for n in order], groups)
 
     evens = list(range(2, cols, 2))
     carried, direct = {0: extra_tile}, {}
@@ -470,30 +504,31 @@
         else:
             carried[m | bit] = local(swap(carried[m], (0, bit), sizes))
 
-    soon, late = list(range(1, cols // 2)), list(range(cols // 2, cols))
-    soon, late = soon + late[-2:], late[:-2]
-    spots = soon + [cols + m for m in evens]
-    sources = [direct[m] for m in soon] + [carried[m] for m in evens]
-    ladder = place(spots, crowded, positions, sources, ladder)
+    order = [m for c, m in hops(cols) if c is None and m]
+    soon, late = order[:-2], order[-2:]
+    spots = soon + [cols + m for m in evens] + [2 * cols]
+    sources = [direct[m] for m in soon] + [carried[m] for m in evens] + [last]
+    ladder = place(spots, positions, sources, ladder)
 
     def again(state):
         return state[0] > 1
 
     def send_seconds(state):
-        mine, other = gather_all(make_block(destination, integral_tiles, cols), sizes)
-        table = make_table(destination, integral_list, cols)
         masked = mask_amplitudes(live_tiles, amplitudes, pair_rows, width)
-        total = contract_mine(table, masked, mine, shape)
+        gathered, came = gather_all(make_block(destination, integral_tiles, cols), sizes)
+        table = make_table(destination, integral_list.T, cols)
+        parts = [(0, n) for n in came]
+        total = contract_all(table, masked, gathered, parts, shape)
         again = [cols + 4 + m for m in slots]
-        *outs, _ = contract_rest(again, [], table, masked, other, total, shape)
+        parts = [(1, n) for n in came]
+        *outs, _ = contract_rest(again, [], table, masked, gathered, parts, total, shape)
         outs = [local(swap(out, (0, m), sizes)) for m, out in zip(slots, outs)]
         spots = list(range(cols + 1, 2 * cols))
-        return jnp.zeros_like(state[0]), place(spots, crowded, positions, outs, state[1])
+        return jnp.zeros_like(state[0]), place(spots, positions, outs, state[1])
 
     ladder = lax.while_loop(again, send_seconds, (crowded[0], ladder))[1]
 
-    sources = [direct[m] for m in late] + [last]
-    return place(late + [2 * cols], crowded, positions, sources, ladder, 2 * cols)
+    return place(late, positions, [direct[m] for m in late], ladder)
 
 
 def solution(mesh):

time: 69.7 us -> 66.1 us (0.948)
  waiting for transfers between devices: 29.7 us -> 21.7 us
  starting transfers between devices: 24.8 us -> 32.2 us
  other arithmetic: 1.45 us -> 0 us
  local copies, waits for them, and re-layouts: 0.78 us -> 0.02 us
    ppermute x21, waiting for transfers between devices: 29.7 us -> 21.7 us  [swap(): return lax.ppermute(value, ('row', 'col'), pairs)]
    ppermute x21, starting transfers between devices: 24.8 us -> 32.2 us  [swap(): return lax.ppermute(value, ('row', 'col'), pairs)]
    concatenate x1 -> x0, other arithmetic: 0.76 us -> none  [make_block(): return jnp.concatenate([integral_tiles, meta], axis=1)]
    unnamed x7 -> x8, local copies, waits for them, and re-layouts: 0.78 us -> 0.02 us
    pallas_call x8 -> x10, Pallas kernels: 7.74 us -> 7.23 us  [the longest x2 2.29 us: contract_all(): pl.pallas_call(functools.partial(contract_all_kernel, parts, total is Non...]
  transfers between devices with their start and end apart: 21 -> 21, of which waited for: 10 -> 10; matrix products, arithmetic and copies ran while one was open for 1% -> 0% of each run, Pallas kernels for 10% -> 14%
where the time goes in v2:
time: 66.1 us; the launch traced here: 65.9 us
  starting transfers between devices  32.2 us (49%)
  waiting for transfers between devices  21.7 us (33%)
  Pallas kernels  11.2 us (17%)
    ppermute x21, starting transfers between devices, swap(): return lax.ppermute(value, ('row', 'col'), pairs)  32.2 us
    ppermute x21, waiting for transfers between devices, swap(): return lax.ppermute(value, ('row', 'col'), pairs)  21.7 us
    pallas_call x1, Pallas kernels, mask_amplitudes(): pl.pallas_call(functools.partial(mask_kernel, pair_rows, width), out_shap...  3.07 us
    pallas_call x2, Pallas kernels, contract_all(): pl.pallas_call(functools.partial(contract_all_kernel, parts, total is Non...  2.29 us
    pallas_call x2, Pallas kernels, place(): pl.pallas_call(functools.partial(place_kernel, places), out_shape=pltpu.H...  1.68 us
  transfers between devices with their start and end apart: 21, of which 10 were waited for; matrix products, arithmetic and copies ran while one was open for 0% of the time, Pallas kernels for 14%

profile of v2, /device:TPU:0, one launch (start us, length us, event | category | flops | bytes accessed | tf_op | source)
XLA Modules:
  0.0 65.9 jit_solution(16472177233753340984)
XLA Ops:
  0.8 5.1 %collective-permute-start.19 = (bf16[1,144,128]{2,1,0:T(8,128)(2,1)S(1)}, bf16[1,144,128]{2,1,0:T(8,128)(2,1)S(1)}, u32[]{:S(2)}, u32[]{:S(2)}) collective-permute-start(bf16[1,144,128]{2,1,0:T(8,128)(2,1)S(1)} %block.3.refs_0_), channel_id=1, source_target_pairs={{0,6},{1,7},{2,4},{3,5},{4,2},{5,3},{6,0},{7,1},{8,14},{9,15},{10,... | collective-permute-start | bytes 110600 | tf_op jit(solution)/shard_map/ppermute | solution.py:32
  6.5 1.3 %collective-permute-done.19.refs_3_ = bf16[1,144,128]{2,1,0:T(8,128)(2,1)S(1)} collective-permute-done((bf16[1,144,128]{2,1,0:T(8,128)(2,1)S(1)}, bf16[1,144,128]{2,1,0:T(8,128)(2,1)S(1)}, u32[]{:S(2)}, u32[]{:S(2)}) %collective-permute-start.19) | collective-permute-done | bytes 36896 | tf_op jit(solution)/shard_map/ppermute | solution.py:32
  7.8 2.9 %collective-permute-done.18.refs_2_ = bf16[1,144,128]{2,1,0:T(8,128)(2,1)S(1)} collective-permute-done((bf16[1,144,128]{2,1,0:T(8,128)(2,1)S(1)}, bf16[1,144,128]{2,1,0:T(8,128)(2,1)S(1)}, u32[]{:S(2)}, u32[]{:S(2)}) %collective-permute-start.18) | collective-permute-done | bytes 36896 | tf_op jit(solution)/shard_map/ppermute | solution.py:32
  10.7 2.5 %collective-permute-start.22 = (bf16[528,128]{1,0:T(8,128)(2,1)S(1)}, bf16[528,128]{1,0:T(8,128)(2,1)S(1)}, u32[]{:S(2)}, u32[]{:S(2)}) collective-permute-start(bf16[528,128]{1,0:T(8,128)(2,1)S(1)} %join.3.refs_0_.rest_0_), channel_id=1, source_target_pairs={{0,17},{1,16},{2,19},{3,18},{4,21},{5,20},{6,23},{7,22},{8,25},{9,... | collective-permute-start | bytes 405512 | tf_op jit(solution)/shard_map/ppermute | solution.py:32
  14.3 2.8 %collective-permute-done.22.refs_3_.rest_1_ = bf16[528,128]{1,0:T(8,128)(2,1)S(1)} collective-permute-done((bf16[528,128]{1,0:T(8,128)(2,1)S(1)}, bf16[528,128]{1,0:T(8,128)(2,1)S(1)}, u32[]{:S(2)}, u32[]{:S(2)}) %collective-permute-start.22) | collective-permute-done | bytes 135200 | tf_op jit(solution)/shard_map/ppermute | solution.py:32
  17.1 1.4 %collective-permute-done.21.refs_2_.rest_0_ = bf16[528,128]{1,0:T(8,128)(2,1)S(1)} collective-permute-done((bf16[528,128]{1,0:T(8,128)(2,1)S(1)}, bf16[528,128]{1,0:T(8,128)(2,1)S(1)}, u32[]{:S(2)}, u32[]{:S(2)}) %collective-permute-start.21) | collective-permute-done | bytes 135200 | tf_op jit(solution)/shard_map/ppermute | solution.py:32
  19.9 3.1 %mask.3.amp = bf16[512,4096]{1,0:T(8,128)(2,1)S(1)} custom-call(s32[8,32]{1,0:T(8,128)} %live.1, bf16[512,4096]{1,0:T(8,128)(2,1)} %amp.1), custom_call_target="tpu_custom_call" | custom-call | tf_op jit(solution)/shard_map/mask/pallas_call | solution.py:133
  23.0 0.9 %contract_all.4.rest_4_ = f32[512,1024]{1,0:T(8,128)S(1)} custom-call(s32[92]{0:T(128)S(4)} %table.3, bf16[512,4096]{1,0:T(8,128)(2,1)S(1)} %mask.3.amp, bf16[528,128]{1,0:T(8,128)(2,1)S(1)} %join.3.refs_0_.rest_0_, bf16[528,128]{1,0:T(8,128)(2,1)S(1)} %collective-permute-done.22.refs_3_.rest_1_), custom_call_target="tpu_custom_call" | custom-call | tf_op jit(solution)/shard_map/contract_all/pallas_call | solution.py:208
  23.9 1.4 %contract_all.5.given = f32[512,1024]{1,0:T(8,128)S(1)} custom-call(s32[92]{0:T(128)S(4)} %table.3, bf16[512,4096]{1,0:T(8,128)(2,1)S(1)} %mask.3.amp, bf16[528,128]{1,0:T(8,128)(2,1)S(1)} %collective-permute-done.21.refs_2_.rest_0_, bf16[528,128]{1,0:T(8,128)(2,1)S(1)} %collective-permute-done.20.refs_1_.rest_1_, ...), custom_call_target="tpu_custom_call", output_to_operand_aliasing={{}: (6, {})} | custom-call | tf_op jit(solution)/shard_map/contract_all/pallas_call | solution.py:208
  25.6 2.1 %collective-permute-start.35 = (bf16[64,1024]{1,0:T(8,128)(2,1)S(1)}, bf16[64,1024]{1,0:T(8,128)(2,1)S(1)}, u32[]{:S(2)}, u32[]{:S(2)}) collective-permute-start(bf16[64,1024]{1,0:T(8,128)(2,1)S(1)} %get-tuple-element.74.rest_0_), channel_id=1, source_target_pairs={{0,4},{1,5},{2,6},{3,7},{4,0},{5,1},{6,2},{7,3},{8,12},{9,13},{10,... | collective-permute-start | bytes 393224 | tf_op jit(solution)/shard_map/ppermute | solution.py:32
  28.1 6.4 %collective-permute-done.35.rest_2_.rest_6_ = bf16[64,1024]{1,0:T(8,128)(2,1)S(1)} collective-permute-done((bf16[64,1024]{1,0:T(8,128)(2,1)S(1)}, bf16[64,1024]{1,0:T(8,128)(2,1)S(1)}, u32[]{:S(2)}, u32[]{:S(2)}) %collective-permute-start.35) | collective-permute-done | bytes 131104 | tf_op jit(solution)/shard_map/ppermute | solution.py:32
  34.5 0.9 %contract_rest.3 = (bf16[64,1024]{1,0:T(8,128)(2,1)S(1)}, bf16[64,1024]{1,0:T(8,128)(2,1)S(1)}, bf16[64,1024]{1,0:T(8,128)(2,1)S(1)}, bf16[64,1024]{1,0:T(8,128)...) custom-call(s32[92]{0:T(128)S(4)} %table.3, ...), custom_call_target="tpu_custom_call", output_to_operand_aliasing={{7}: (2, {})} | custom-call | tf_op jit(solution)/shard_map/contract_rest/pallas_call | solution.py:243
  35.4 3.7 %collective-permute-start.29 = (bf16[64,1024]{1,0:T(8,128)(2,1)S(1)}, bf16[64,1024]{1,0:T(8,128)(2,1)S(1)}, u32[]{:S(2)}, u32[]{:S(2)}) collective-permute-start(bf16[64,1024]{1,0:T(8,128)(2,1)S(1)} %get-tuple-element.69), channel_id=1, source_target_pairs={{0,7},{1,6},{2,5},{3,4},{4,3},{5,2},{6,1},{7,0},{8,15},{9,14},{10,... | collective-permute-start | bytes 393224 | tf_op jit(solution)/shard_map/ppermute | solution.py:32
  39.7 1.0 %collective-permute-start.31 = (bf16[64,1024]{1,0:T(8,128)(2,1)S(1)}, bf16[64,1024]{1,0:T(8,128)(2,1)S(1)}, u32[]{:S(2)}, u32[]{:S(2)}) collective-permute-start(bf16[64,1024]{1,0:T(8,128)(2,1)S(1)} %get-tuple-element.71), channel_id=1, source_target_pairs={{0,6},{1,7},{2,4},{3,5},{4,2},{5,3},{6,0},{7,1},{8,14},{9,15},{10,... | collective-permute-start | bytes 393224 | tf_op jit(solution)/shard_map/ppermute | solution.py:32
  41.3 1.7 %collective-permute-start.32 = (bf16[64,1024]{1,0:T(8,128)(2,1)S(1)}, bf16[64,1024]{1,0:T(8,128)(2,1)S(1)}, u32[]{:S(2)}, u32[]{:S(2)}) collective-permute-start(bf16[64,1024]{1,0:T(8,128)(2,1)S(1)} %get-tuple-element.72), channel_id=1, source_target_pairs={{0,3},{1,2},{2,1},{3,0},{4,7},{5,6},{6,5},{7,4},{8,11},{9,10},{10,... | collective-permute-start | bytes 393224 | tf_op jit(solution)/shard_map/ppermute | solution.py:32
  43.0 2.6 %collective-permute-start.33 = (bf16[64,1024]{1,0:T(8,128)(2,1)S(1)}, bf16[64,1024]{1,0:T(8,128)(2,1)S(1)}, u32[]{:S(2)}, u32[]{:S(2)}) collective-permute-start(bf16[64,1024]{1,0:T(8,128)(2,1)S(1)} %get-tuple-element.73), channel_id=1, source_target_pairs={{0,5},{1,4},{2,7},{3,6},{4,1},{5,0},{6,3},{7,2},{8,13},{9,12},{10,... | collective-permute-start | bytes 393224 | tf_op jit(solution)/shard_map/ppermute | solution.py:32
  45.6 1.5 %collective-permute-start.37 = (bf16[64,1024]{1,0:T(8,128)(2,1)S(1)}, bf16[64,1024]{1,0:T(8,128)(2,1)S(1)}, u32[]{:S(2)}, u32[]{:S(2)}) collective-permute-start(bf16[64,1024]{1,0:T(8,128)(2,1)S(1)} %choose.1), channel_id=1, source_target_pairs={{0,1},{1,0},{2,3},{3,2},{4,5},{5,4},{6,7},{7,6},{8,9},{9,8},{10,11... | collective-permute-start | bytes 393224 | tf_op jit(solution)/shard_map/ppermute | solution.py:32
  47.1 1.7 %collective-permute-done.30.rest_1_ = bf16[64,1024]{1,0:T(8,128)(2,1)S(1)} collective-permute-done((bf16[64,1024]{1,0:T(8,128)(2,1)S(1)}, bf16[64,1024]{1,0:T(8,128)(2,1)S(1)}, u32[]{:S(2)}, u32[]{:S(2)}) %collective-permute-start.30) | collective-permute-done | bytes 131104 | tf_op jit(solution)/shard_map/ppermute | solution.py:32
  48.8 7.2 %collective-permute-start.27 = (bf16[64,1024]{1,0:T(8,128)(2,1)S(1)}, bf16[64,1024]{1,0:T(8,128)(2,1)S(1)}, u32[]{:S(2)}, u32[]{:S(2)}) collective-permute-start(bf16[64,1024]{1,0:T(8,128)(2,1)S(1)} %get-tuple-element.67), channel_id=1, source_target_pairs={{0,2},{1,3},{2,0},{3,1},{4,6},{5,7},{6,4},{7,5},{8,10},{9,11},{10,... | collective-permute-start | bytes 393224 | tf_op jit(solution)/shard_map/ppermute | solution.py:32
  56.0 1.8 %collective-permute-start.28 = (bf16[64,1024]{1,0:T(8,128)(2,1)S(1)}, bf16[64,1024]{1,0:T(8,128)(2,1)S(1)}, u32[]{:S(2)}, u32[]{:S(2)}) collective-permute-start(bf16[64,1024]{1,0:T(8,128)(2,1)S(1)} %get-tuple-element.68), channel_id=1, source_target_pairs={{0,4},{1,5},{2,6},{3,7},{4,0},{5,1},{6,2},{7,3},{8,12},{9,13},{10,... | collective-permute-start | bytes 393224 | tf_op jit(solution)/shard_map/ppermute | solution.py:32
  57.8 0.9 %crowding.1 = s32[1]{0:T(128)} custom-call(bf16[528,128]{1,0:T(8,128)(2,1)S(1)} %join.3.refs_0_.rest_0_, bf16[528,128]{1,0:T(8,128)(2,1)S(1)} %collective-permute-done.20.refs_1_.rest_1_, bf16[528,128]{1,0:T(8,128)(2,1)S(1)} %collective-permute-done.21.refs_2_.rest_0_, bf16[528,128]{1,0:T(8,128)(2,1)S(1)} %collective-permute-done.22.refs_3_.rest_1_, ...), custom_call_target="tpu_custom_call" | custom-call | tf_op jit(solution)/shard_map/crowding/pallas_call | solution.py:391
  58.7 1.2 %collective-permute-done.33.rest_4_ = bf16[64,1024]{1,0:T(8,128)(2,1)S(1)} collective-permute-done((bf16[64,1024]{1,0:T(8,128)(2,1)S(1)}, bf16[64,1024]{1,0:T(8,128)(2,1)S(1)}, u32[]{:S(2)}, u32[]{:S(2)}) %collective-permute-start.33) | collective-permute-done | bytes 131104 | tf_op jit(solution)/shard_map/ppermute | solution.py:32
  59.9 0.9 %place.4 = bf16[512,1024]{1,0:T(8,128)(2,1)} custom-call(s32[17]{0:T(128)S(4)} %get-tuple-element.109.positions, bf16[64,1024]{1,0:T(8,128)(2,1)S(1)} %collective-permute-done.29.rest_0_, bf16[64,1024]{1,0:T(8,128)(2,1)S(1)} %collective-permute-done.30.rest_1_, ...), custom_call_target="tpu_custom_call", output_to_operand_aliasing={{}: (10, {})} | custom-call | tf_op jit(solution)/shard_map/place/pallas_call | solution.py:438
  61.5 3.0 %collective-permute-done.28.rest_1_ = bf16[64,1024]{1,0:T(8,128)(2,1)S(1)} collective-permute-done((bf16[64,1024]{1,0:T(8,128)(2,1)S(1)}, bf16[64,1024]{1,0:T(8,128)(2,1)S(1)}, u32[]{:S(2)}, u32[]{:S(2)}) %collective-permute-start.28) | collective-permute-done | bytes 131104 | tf_op jit(solution)/shard_map/ppermute | solution.py:32
  (40 shorter events, 7.5 us)
Async XLA Ops:
  0.8 7.0 %collective-permute-start.19 = (bf16[1,144,128]{2,1,0:T(8,128)(2,1)S(1)}, bf16[1,144,128]{2,1,0:T(8,128)(2,1)S(1)}, u32[]{:S(2)}, u32[]{:S(2)}) collective-permute-start(bf16[1,144,128]{2,1,0:T(8,128)(2,1)S(1)} %block.3.refs_0_), channel_id=1, source_target_pairs={{0,6},{1,7},{2,4},{3,5},{4,2},{5,3},{6,0},{7,1},{8,14},{9,15},{10,... | collective-permute-start | bytes 110600 | tf_op jit(solution)/shard_map/ppermute | solution.py:32
  5.9 4.9 %collective-permute-start.18 = (bf16[1,144,128]{2,1,0:T(8,128)(2,1)S(1)}, bf16[1,144,128]{2,1,0:T(8,128)(2,1)S(1)}, u32[]{:S(2)}, u32[]{:S(2)}) collective-permute-start(bf16[1,144,128]{2,1,0:T(8,128)(2,1)S(1)} %block.3.refs_0_), channel_id=1, source_target_pairs={{0,4},{1,5},{2,6},{3,7},{4,0},{5,1},{6,2},{7,3},{8,12},{9,13},{10,... | collective-permute-start | bytes 110600 | tf_op jit(solution)/shard_map/ppermute | solution.py:32
  5.9 4.9 %collective-permute-start.17 = (bf16[1,144,128]{2,1,0:T(8,128)(2,1)S(1)}, bf16[1,144,128]{2,1,0:T(8,128)(2,1)S(1)}, u32[]{:S(2)}, u32[]{:S(2)}) collective-permute-start(bf16[1,144,128]{2,1,0:T(8,128)(2,1)S(1)} %block.3.refs_0_), channel_id=1, source_target_pairs={{0,2},{1,3},{2,0},{3,1},{4,6},{5,7},{6,4},{7,5},{8,10},{9,11},{10,... | collective-permute-start | bytes 110600 | tf_op jit(solution)/shard_map/ppermute | solution.py:32
  10.7 6.4 %collective-permute-start.22 = (bf16[528,128]{1,0:T(8,128)(2,1)S(1)}, bf16[528,128]{1,0:T(8,128)(2,1)S(1)}, u32[]{:S(2)}, u32[]{:S(2)}) collective-permute-start(bf16[528,128]{1,0:T(8,128)(2,1)S(1)} %join.3.refs_0_.rest_0_), channel_id=1, source_target_pairs={{0,17},{1,16},{2,19},{3,18},{4,21},{5,20},{6,23},{7,22},{8,25},{9,... | collective-permute-start | bytes 405512 | tf_op jit(solution)/shard_map/ppermute | solution.py:32
  13.3 5.3 %collective-permute-start.21 = (bf16[528,128]{1,0:T(8,128)(2,1)S(1)}, bf16[528,128]{1,0:T(8,128)(2,1)S(1)}, u32[]{:S(2)}, u32[]{:S(2)}) collective-permute-start(bf16[528,128]{1,0:T(8,128)(2,1)S(1)} %join.3.refs_0_.rest_0_), channel_id=1, source_target_pairs={{0,16},{1,17},{2,18},{3,19},{4,20},{5,21},{6,22},{7,23},{8,24},{9,... | collective-permute-start | bytes 405512 | tf_op jit(solution)/shard_map/ppermute | solution.py:32
  13.8 5.0 %collective-permute-start.20 = (bf16[528,128]{1,0:T(8,128)(2,1)S(1)}, bf16[528,128]{1,0:T(8,128)(2,1)S(1)}, u32[]{:S(2)}, u32[]{:S(2)}) collective-permute-start(bf16[528,128]{1,0:T(8,128)(2,1)S(1)} %join.3.refs_0_.rest_0_), channel_id=1, source_target_pairs={{0,1},{1,0},{2,3},{3,2},{4,5},{5,4},{6,7},{7,6},{8,9},{9,8},{10,11... | collective-permute-start | bytes 405512 | tf_op jit(solution)/shard_map/ppermute | solution.py:32
  14.3 9.6 %collective-permute-start.23 = (bf16[528,128]{1,0:T(8,128)(2,1)S(1)}, bf16[528,128]{1,0:T(8,128)(2,1)S(1)}, u32[]{:S(2)}, u32[]{:S(2)}) collective-permute-start(bf16[528,128]{1,0:T(8,128)(2,1)S(1)} %join.3.refs_0_.rest_0_), channel_id=1, source_target_pairs={{0,8},{1,9},{2,10},{3,11},{4,12},{5,13},{6,14},{7,15},{8,0},{9,1},... | collective-permute-start | bytes 405512 | tf_op jit(solution)/shard_map/ppermute | solution.py:32
  17.1 6.7 %collective-permute-start.24 = (bf16[528,128]{1,0:T(8,128)(2,1)S(1)}, bf16[528,128]{1,0:T(8,128)(2,1)S(1)}, u32[]{:S(2)}, u32[]{:S(2)}) collective-permute-start(bf16[528,128]{1,0:T(8,128)(2,1)S(1)} %collective-permute-done.22.refs_3_.rest_1_), channel_id=1, source_target_pairs={{0,8},{1,9},{2,10},{3,11},{4,12},{5,13},{6,14},{7,15},{8,0},{9,1},... | collective-permute-start | bytes 405512 | tf_op jit(solution)/shard_map/ppermute | solution.py:32
  18.6 6.8 %collective-permute-start.25 = (bf16[528,128]{1,0:T(8,128)(2,1)S(1)}, bf16[528,128]{1,0:T(8,128)(2,1)S(1)}, u32[]{:S(2)}, u32[]{:S(2)}) collective-permute-start(bf16[528,128]{1,0:T(8,128)(2,1)S(1)} %collective-permute-done.21.refs_2_.rest_0_), channel_id=1, source_target_pairs={{0,8},{1,9},{2,10},{3,11},{4,12},{5,13},{6,14},{7,15},{8,0},{9,1},... | collective-permute-start | bytes 405512 | tf_op jit(solution)/shard_map/ppermute | solution.py:32
  18.8 6.5 %collective-permute-start.26 = (bf16[528,128]{1,0:T(8,128)(2,1)S(1)}, bf16[528,128]{1,0:T(8,128)(2,1)S(1)}, u32[]{:S(2)}, u32[]{:S(2)}) collective-permute-start(bf16[528,128]{1,0:T(8,128)(2,1)S(1)} %collective-permute-done.20.refs_1_.rest_1_), channel_id=1, source_target_pairs={{0,8},{1,9},{2,10},{3,11},{4,12},{5,13},{6,14},{7,15},{8,0},{9,1},... | collective-permute-start | bytes 405512 | tf_op jit(solution)/shard_map/ppermute | solution.py:32
  25.6 8.9 %collective-permute-start.35 = (bf16[64,1024]{1,0:T(8,128)(2,1)S(1)}, bf16[64,1024]{1,0:T(8,128)(2,1)S(1)}, u32[]{:S(2)}, u32[]{:S(2)}) collective-permute-start(bf16[64,1024]{1,0:T(8,128)(2,1)S(1)} %get-tuple-element.74.rest_0_), channel_id=1, source_target_pairs={{0,4},{1,5},{2,6},{3,7},{4,0},{5,1},{6,2},{7,3},{8,12},{9,13},{10,... | collective-permute-start | bytes 393224 | tf_op jit(solution)/shard_map/ppermute | solution.py:32
  27.7 13.6 %collective-permute-start.34 = (bf16[64,1024]{1,0:T(8,128)(2,1)S(1)}, bf16[64,1024]{1,0:T(8,128)(2,1)S(1)}, u32[]{:S(2)}, u32[]{:S(2)}) collective-permute-start(bf16[64,1024]{1,0:T(8,128)(2,1)S(1)} %get-tuple-element.74.rest_0_), channel_id=1, source_target_pairs={{0,2},{1,3},{2,0},{3,1},{4,6},{5,7},{6,4},{7,5},{8,10},{9,11},{10,... | collective-permute-start | bytes 393224 | tf_op jit(solution)/shard_map/ppermute | solution.py:32
  34.5 8.5 %collective-permute-start.36 = (bf16[64,1024]{1,0:T(8,128)(2,1)S(1)}, bf16[64,1024]{1,0:T(8,128)(2,1)S(1)}, u32[]{:S(2)}, u32[]{:S(2)}) collective-permute-start(bf16[64,1024]{1,0:T(8,128)(2,1)S(1)} %collective-permute-done.35.rest_2_.rest_6_), channel_id=1, source_target_pairs={{0,2},{1,3},{2,0},{3,1},{4,6},{5,7},{6,4},{7,5},{8,10},{9,11},{10,... | collective-permute-start | bytes 393224 | tf_op jit(solution)/shard_map/ppermute | solution.py:32
  35.4 10.2 %collective-permute-start.29 = (bf16[64,1024]{1,0:T(8,128)(2,1)S(1)}, bf16[64,1024]{1,0:T(8,128)(2,1)S(1)}, u32[]{:S(2)}, u32[]{:S(2)}) collective-permute-start(bf16[64,1024]{1,0:T(8,128)(2,1)S(1)} %get-tuple-element.69), channel_id=1, source_target_pairs={{0,7},{1,6},{2,5},{3,4},{4,3},{5,2},{6,1},{7,0},{8,15},{9,14},{10,... | collective-permute-start | bytes 393224 | tf_op jit(solution)/shard_map/ppermute | solution.py:32
  39.2 9.6 %collective-permute-start.30 = (bf16[64,1024]{1,0:T(8,128)(2,1)S(1)}, bf16[64,1024]{1,0:T(8,128)(2,1)S(1)}, u32[]{:S(2)}, u32[]{:S(2)}) collective-permute-start(bf16[64,1024]{1,0:T(8,128)(2,1)S(1)} %get-tuple-element.70), channel_id=1, source_target_pairs={{0,1},{1,0},{2,3},{3,2},{4,5},{5,4},{6,7},{7,6},{8,9},{9,8},{10,11... | collective-permute-start | bytes 393224 | tf_op jit(solution)/shard_map/ppermute | solution.py:32
  39.7 16.3 %collective-permute-start.31 = (bf16[64,1024]{1,0:T(8,128)(2,1)S(1)}, bf16[64,1024]{1,0:T(8,128)(2,1)S(1)}, u32[]{:S(2)}, u32[]{:S(2)}) collective-permute-start(bf16[64,1024]{1,0:T(8,128)(2,1)S(1)} %get-tuple-element.71), channel_id=1, source_target_pairs={{0,6},{1,7},{2,4},{3,5},{4,2},{5,3},{6,0},{7,1},{8,14},{9,15},{10,... | collective-permute-start | bytes 393224 | tf_op jit(solution)/shard_map/ppermute | solution.py:32
  41.3 17.4 %collective-permute-start.32 = (bf16[64,1024]{1,0:T(8,128)(2,1)S(1)}, bf16[64,1024]{1,0:T(8,128)(2,1)S(1)}, u32[]{:S(2)}, u32[]{:S(2)}) collective-permute-start(bf16[64,1024]{1,0:T(8,128)(2,1)S(1)} %get-tuple-element.72), channel_id=1, source_target_pairs={{0,3},{1,2},{2,1},{3,0},{4,7},{5,6},{6,5},{7,4},{8,11},{9,10},{10,... | collective-permute-start | bytes 393224 | tf_op jit(solution)/shard_map/ppermute | solution.py:32
  43.0 16.9 %collective-permute-start.33 = (bf16[64,1024]{1,0:T(8,128)(2,1)S(1)}, bf16[64,1024]{1,0:T(8,128)(2,1)S(1)}, u32[]{:S(2)}, u32[]{:S(2)}) collective-permute-start(bf16[64,1024]{1,0:T(8,128)(2,1)S(1)} %get-tuple-element.73), channel_id=1, source_target_pairs={{0,5},{1,4},{2,7},{3,6},{4,1},{5,0},{6,3},{7,2},{8,13},{9,12},{10,... | collective-permute-start | bytes 393224 | tf_op jit(solution)/shard_map/ppermute | solution.py:32
  45.6 14.3 %collective-permute-start.37 = (bf16[64,1024]{1,0:T(8,128)(2,1)S(1)}, bf16[64,1024]{1,0:T(8,128)(2,1)S(1)}, u32[]{:S(2)}, u32[]{:S(2)}) collective-permute-start(bf16[64,1024]{1,0:T(8,128)(2,1)S(1)} %choose.1), channel_id=1, source_target_pairs={{0,1},{1,0},{2,3},{3,2},{4,5},{5,4},{6,7},{7,6},{8,9},{9,8},{10,11... | collective-permute-start | bytes 393224 | tf_op jit(solution)/shard_map/ppermute | solution.py:32
  48.8 12.7 %collective-permute-start.27 = (bf16[64,1024]{1,0:T(8,128)(2,1)S(1)}, bf16[64,1024]{1,0:T(8,128)(2,1)S(1)}, u32[]{:S(2)}, u32[]{:S(2)}) collective-permute-start(bf16[64,1024]{1,0:T(8,128)(2,1)S(1)} %get-tuple-element.67), channel_id=1, source_target_pairs={{0,2},{1,3},{2,0},{3,1},{4,6},{5,7},{6,4},{7,5},{8,10},{9,11},{10,... | collective-permute-start | bytes 393224 | tf_op jit(solution)/shard_map/ppermute | solution.py:32
  56.0 8.5 %copy-start = (bf16[1,128,128]{2,1,0:T(8,128)(2,1)S(1)}, bf16[1,128,128]{2,1,0:T(8,128)(2,1)}, u32[]{:S(2)}) copy-start(bf16[1,128,128]{2,1,0:T(8,128)(2,1)} %integrals.1) | copy-start | bytes 98308
  56.0 8.5 %copy-start.1 = (s32[8,32]{1,0:T(8,128)S(1)}, s32[8,32]{1,0:T(8,128)}, u32[]{:S(2)}) copy-start(s32[8,32]{1,0:T(8,128)} %live.1) | copy-start | bytes 3076
  56.0 8.5 %copy-start.2 = (s32[8]{0:T(128)S(1)}, s32[8]{0:T(128)}, u32[]{:S(2)}) copy-start(s32[8]{0:T(128)} %destination.1) | copy-start | bytes 100
  56.0 8.5 %collective-permute-start.28 = (bf16[64,1024]{1,0:T(8,128)(2,1)S(1)}, bf16[64,1024]{1,0:T(8,128)(2,1)S(1)}, u32[]{:S(2)}, u32[]{:S(2)}) collective-permute-start(bf16[64,1024]{1,0:T(8,128)(2,1)S(1)} %get-tuple-element.68), channel_id=1, source_target_pairs={{0,4},{1,5},{2,6},{3,7},{4,0},{5,1},{6,2},{7,3},{8,12},{9,13},{10,... | collective-permute-start | bytes 393224 | tf_op jit(solution)/shard_map/ppermute | solution.py:32
  (1 other events, 8.5 us)

commit v3 on v2

--- a/solution.py
+++ b/solution.py
@@ -475,11 +475,14 @@
     gathered, came = gather_all(make_block(destination, integral_tiles, cols), sizes)
     table = make_table(destination, integral_list.T, cols)
     shape = (pair_rows, held_tiles, cols)
-    soon, late = came[: len(came) // 2], came[len(came) // 2 :]
-    total = contract_all(table, masked, gathered, [(0, n) for n in soon], shape)
-    parts = [(0, n) for n in late] + [(1, n) for n in soon]
-    total = contract_all(table, masked, gathered, parts, shape, total)
-    parts = [(1, n) for n in late]
+    steps = [came[:1], came[1 : len(came) // 2], came[len(came) // 2 : -1], came[-1:]]
+    total = None
+    for mine, theirs in (
+        (steps[0], steps[0]), (steps[1], steps[1]), (steps[2] + steps[3], steps[2])
+    ):
+        parts = [(0, n) for n in mine] + [(1, n) for n in theirs]
+        total = contract_all(table, masked, gathered, parts, shape, total)
+    parts = [(1, n) for n in steps[3]]
     extra_tile, total = contract_one(cols + 1, table, masked, gathered, parts, total, shape)
     slots = list(range(1, cols))
     own = [(0, cols + 2), (cols, cols + 3)]

time: 66.1 us -> 66.2 us (level)
    pallas_call x2 -> x3, Pallas kernels: 2.29 us -> 2.73 us  [contract_all(): pl.pallas_call(functools.partial(contract_all_kernel, parts, total is Non...]
where the time goes in v3:
time: 66.2 us; the launch traced here: 66 us
  starting transfers between devices  32.2 us (49%)
  waiting for transfers between devices  21.7 us (33%)
  Pallas kernels  11.2 us (17%)
    ppermute x21, starting transfers between devices, swap(): return lax.ppermute(value, ('row', 'col'), pairs)  32.2 us
    ppermute x21, waiting for transfers between devices, swap(): return lax.ppermute(value, ('row', 'col'), pairs)  21.7 us
    pallas_call x1, Pallas kernels, mask_amplitudes(): pl.pallas_call(functools.partial(mask_kernel, pair_rows, width), out_shap...  3.07 us
    pallas_call x3, Pallas kernels, contract_all(): pl.pallas_call(functools.partial(contract_all_kernel, parts, total is Non...  2.73 us
    pallas_call x2, Pallas kernels, place(): pl.pallas_call(functools.partial(place_kernel, places), out_shape=pltpu.H...  1.68 us
  transfers between devices with their start and end apart: 21, of which 10 were waited for; matrix products, arithmetic and copies ran while one was open for 0% of the time, Pallas kernels for 14%

profile of v3, /device:TPU:0, one launch (start us, length us, event | category | flops | bytes accessed | tf_op | source)
XLA Modules:
  0.0 66.0 jit_solution(9450035239033163097)
XLA Ops:
  0.8 5.1 %collective-permute-start.19 = (bf16[1,144,128]{2,1,0:T(8,128)(2,1)S(1)}, bf16[1,144,128]{2,1,0:T(8,128)(2,1)S(1)}, u32[]{:S(2)}, u32[]{:S(2)}) collective-permute-start(bf16[1,144,128]{2,1,0:T(8,128)(2,1)S(1)} %block.3.refs_0_), channel_id=1, source_target_pairs={{0,6},{1,7},{2,4},{3,5},{4,2},{5,3},{6,0},{7,1},{8,14},{9,15},{10,... | collective-permute-start | bytes 110600 | tf_op jit(solution)/shard_map/ppermute | solution.py:32
  6.5 1.3 %collective-permute-done.19.refs_3_ = bf16[1,144,128]{2,1,0:T(8,128)(2,1)S(1)} collective-permute-done((bf16[1,144,128]{2,1,0:T(8,128)(2,1)S(1)}, bf16[1,144,128]{2,1,0:T(8,128)(2,1)S(1)}, u32[]{:S(2)}, u32[]{:S(2)}) %collective-permute-start.19) | collective-permute-done | bytes 36896 | tf_op jit(solution)/shard_map/ppermute | solution.py:32
  7.8 2.9 %collective-permute-done.18.refs_2_ = bf16[1,144,128]{2,1,0:T(8,128)(2,1)S(1)} collective-permute-done((bf16[1,144,128]{2,1,0:T(8,128)(2,1)S(1)}, bf16[1,144,128]{2,1,0:T(8,128)(2,1)S(1)}, u32[]{:S(2)}, u32[]{:S(2)}) %collective-permute-start.18) | collective-permute-done | bytes 36896 | tf_op jit(solution)/shard_map/ppermute | solution.py:32
  10.7 2.5 %collective-permute-start.22 = (bf16[528,128]{1,0:T(8,128)(2,1)S(1)}, bf16[528,128]{1,0:T(8,128)(2,1)S(1)}, u32[]{:S(2)}, u32[]{:S(2)}) collective-permute-start(bf16[528,128]{1,0:T(8,128)(2,1)S(1)} %join.3.refs_0_.rest_0_), channel_id=1, source_target_pairs={{0,17},{1,16},{2,19},{3,18},{4,21},{5,20},{6,23},{7,22},{8,25},{9,... | collective-permute-start | bytes 405512 | tf_op jit(solution)/shard_map/ppermute | solution.py:32
  14.3 2.8 %collective-permute-done.22.refs_3_.rest_0_ = bf16[528,128]{1,0:T(8,128)(2,1)S(1)} collective-permute-done((bf16[528,128]{1,0:T(8,128)(2,1)S(1)}, bf16[528,128]{1,0:T(8,128)(2,1)S(1)}, u32[]{:S(2)}, u32[]{:S(2)}) %collective-permute-start.22) | collective-permute-done | bytes 135200 | tf_op jit(solution)/shard_map/ppermute | solution.py:32
  17.1 1.4 %collective-permute-done.21.refs_2_.rest_0_ = bf16[528,128]{1,0:T(8,128)(2,1)S(1)} collective-permute-done((bf16[528,128]{1,0:T(8,128)(2,1)S(1)}, bf16[528,128]{1,0:T(8,128)(2,1)S(1)}, u32[]{:S(2)}, u32[]{:S(2)}) %collective-permute-start.21) | collective-permute-done | bytes 135200 | tf_op jit(solution)/shard_map/ppermute | solution.py:32
  19.1 0.8 %table.3 = s32[92]{0:T(128)S(4)} custom-call(s32[8]{0:T(128)} %destination.1, s32[2,32]{1,0:T(2,128)} %bitcast.7), custom_call_target="tpu_custom_call" | custom-call | tf_op jit(solution)/shard_map/table/pallas_call | solution.py:300
  19.9 3.1 %mask.3.amp = bf16[512,4096]{1,0:T(8,128)(2,1)S(1)} custom-call(s32[8,32]{1,0:T(8,128)} %live.1, bf16[512,4096]{1,0:T(8,128)(2,1)} %amp.1), custom_call_target="tpu_custom_call" | custom-call | tf_op jit(solution)/shard_map/mask/pallas_call | solution.py:133
  23.0 0.9 %contract_all.5.rest_2_ = f32[512,1024]{1,0:T(8,128)S(1)} custom-call(s32[92]{0:T(128)S(4)} %table.3, bf16[512,4096]{1,0:T(8,128)(2,1)S(1)} %mask.3.amp, bf16[528,128]{1,0:T(8,128)(2,1)S(1)} %join.3.refs_0_.rest_0_, bf16[528,128]{1,0:T(8,128)(2,1)S(1)} %collective-permute-done.25.rest_1_.refs_4_), custom_call_target="tpu_custom_call" | custom-call | tf_op jit(solution)/shard_map/contract_all/pallas_call | solution.py:208
  24.7 1.1 %contract_all.7.given = f32[512,1024]{1,0:T(8,128)S(1)} custom-call(s32[92]{0:T(128)S(4)} %table.3, bf16[512,4096]{1,0:T(8,128)(2,1)S(1)} %mask.3.amp, bf16[528,128]{1,0:T(8,128)(2,1)S(1)} %collective-permute-done.21.refs_2_.rest_0_, bf16[528,128]{1,0:T(8,128)(2,1)S(1)} %collective-permute-done.20.refs_1_.rest_1_, ...), custom_call_target="tpu_custom_call", output_to_operand_aliasing={{}: (5, {})} | custom-call | tf_op jit(solution)/shard_map/contract_all/pallas_call | solution.py:208
  26.0 2.1 %collective-permute-start.35 = (bf16[64,1024]{1,0:T(8,128)(2,1)S(1)}, bf16[64,1024]{1,0:T(8,128)(2,1)S(1)}, u32[]{:S(2)}, u32[]{:S(2)}) collective-permute-start(bf16[64,1024]{1,0:T(8,128)(2,1)S(1)} %get-tuple-element.74.rest_0_), channel_id=1, source_target_pairs={{0,4},{1,5},{2,6},{3,7},{4,0},{5,1},{6,2},{7,3},{8,12},{9,13},{10,... | collective-permute-start | bytes 393224 | tf_op jit(solution)/shard_map/ppermute | solution.py:32
  28.5 6.4 %collective-permute-done.35.rest_2_.rest_6_ = bf16[64,1024]{1,0:T(8,128)(2,1)S(1)} collective-permute-done((bf16[64,1024]{1,0:T(8,128)(2,1)S(1)}, bf16[64,1024]{1,0:T(8,128)(2,1)S(1)}, u32[]{:S(2)}, u32[]{:S(2)}) %collective-permute-start.35) | collective-permute-done | bytes 131104 | tf_op jit(solution)/shard_map/ppermute | solution.py:32
  35.5 3.7 %collective-permute-start.29 = (bf16[64,1024]{1,0:T(8,128)(2,1)S(1)}, bf16[64,1024]{1,0:T(8,128)(2,1)S(1)}, u32[]{:S(2)}, u32[]{:S(2)}) collective-permute-start(bf16[64,1024]{1,0:T(8,128)(2,1)S(1)} %get-tuple-element.69), channel_id=1, source_target_pairs={{0,7},{1,6},{2,5},{3,4},{4,3},{5,2},{6,1},{7,0},{8,15},{9,14},{10,... | collective-permute-start | bytes 393224 | tf_op jit(solution)/shard_map/ppermute | solution.py:32
  39.8 1.1 %collective-permute-start.31 = (bf16[64,1024]{1,0:T(8,128)(2,1)S(1)}, bf16[64,1024]{1,0:T(8,128)(2,1)S(1)}, u32[]{:S(2)}, u32[]{:S(2)}) collective-permute-start(bf16[64,1024]{1,0:T(8,128)(2,1)S(1)} %get-tuple-element.71), channel_id=1, source_target_pairs={{0,6},{1,7},{2,4},{3,5},{4,2},{5,3},{6,0},{7,1},{8,14},{9,15},{10,... | collective-permute-start | bytes 393224 | tf_op jit(solution)/shard_map/ppermute | solution.py:32
  41.3 1.7 %collective-permute-start.32 = (bf16[64,1024]{1,0:T(8,128)(2,1)S(1)}, bf16[64,1024]{1,0:T(8,128)(2,1)S(1)}, u32[]{:S(2)}, u32[]{:S(2)}) collective-permute-start(bf16[64,1024]{1,0:T(8,128)(2,1)S(1)} %get-tuple-element.72), channel_id=1, source_target_pairs={{0,3},{1,2},{2,1},{3,0},{4,7},{5,6},{6,5},{7,4},{8,11},{9,10},{10,... | collective-permute-start | bytes 393224 | tf_op jit(solution)/shard_map/ppermute | solution.py:32
  43.1 2.6 %collective-permute-start.33 = (bf16[64,1024]{1,0:T(8,128)(2,1)S(1)}, bf16[64,1024]{1,0:T(8,128)(2,1)S(1)}, u32[]{:S(2)}, u32[]{:S(2)}) collective-permute-start(bf16[64,1024]{1,0:T(8,128)(2,1)S(1)} %get-tuple-element.73), channel_id=1, source_target_pairs={{0,5},{1,4},{2,7},{3,6},{4,1},{5,0},{6,3},{7,2},{8,13},{9,12},{10,... | collective-permute-start | bytes 393224 | tf_op jit(solution)/shard_map/ppermute | solution.py:32
  45.7 1.5 %collective-permute-start.37 = (bf16[64,1024]{1,0:T(8,128)(2,1)S(1)}, bf16[64,1024]{1,0:T(8,128)(2,1)S(1)}, u32[]{:S(2)}, u32[]{:S(2)}) collective-permute-start(bf16[64,1024]{1,0:T(8,128)(2,1)S(1)} %choose.1), channel_id=1, source_target_pairs={{0,1},{1,0},{2,3},{3,2},{4,5},{5,4},{6,7},{7,6},{8,9},{9,8},{10,11... | collective-permute-start | bytes 393224 | tf_op jit(solution)/shard_map/ppermute | solution.py:32
  47.2 1.7 %collective-permute-done.30.rest_1_ = bf16[64,1024]{1,0:T(8,128)(2,1)S(1)} collective-permute-done((bf16[64,1024]{1,0:T(8,128)(2,1)S(1)}, bf16[64,1024]{1,0:T(8,128)(2,1)S(1)}, u32[]{:S(2)}, u32[]{:S(2)}) %collective-permute-start.30) | collective-permute-done | bytes 131104 | tf_op jit(solution)/shard_map/ppermute | solution.py:32
  48.9 7.2 %collective-permute-start.27 = (bf16[64,1024]{1,0:T(8,128)(2,1)S(1)}, bf16[64,1024]{1,0:T(8,128)(2,1)S(1)}, u32[]{:S(2)}, u32[]{:S(2)}) collective-permute-start(bf16[64,1024]{1,0:T(8,128)(2,1)S(1)} %get-tuple-element.67), channel_id=1, source_target_pairs={{0,2},{1,3},{2,0},{3,1},{4,6},{5,7},{6,4},{7,5},{8,10},{9,11},{10,... | collective-permute-start | bytes 393224 | tf_op jit(solution)/shard_map/ppermute | solution.py:32
  56.1 1.8 %collective-permute-start.28 = (bf16[64,1024]{1,0:T(8,128)(2,1)S(1)}, bf16[64,1024]{1,0:T(8,128)(2,1)S(1)}, u32[]{:S(2)}, u32[]{:S(2)}) collective-permute-start(bf16[64,1024]{1,0:T(8,128)(2,1)S(1)} %get-tuple-element.68), channel_id=1, source_target_pairs={{0,4},{1,5},{2,6},{3,7},{4,0},{5,1},{6,2},{7,3},{8,12},{9,13},{10,... | collective-permute-start | bytes 393224 | tf_op jit(solution)/shard_map/ppermute | solution.py:32
  57.9 0.9 %crowding.1 = s32[1]{0:T(128)} custom-call(bf16[528,128]{1,0:T(8,128)(2,1)S(1)} %join.3.refs_0_.rest_0_, bf16[528,128]{1,0:T(8,128)(2,1)S(1)} %collective-permute-done.20.refs_1_.rest_1_, bf16[528,128]{1,0:T(8,128)(2,1)S(1)} %collective-permute-done.21.refs_2_.rest_0_, bf16[528,128]{1,0:T(8,128)(2,1)S(1)} %collective-permute-done.22.refs_3_.rest_0_, ...), custom_call_target="tpu_custom_call" | custom-call | tf_op jit(solution)/shard_map/crowding/pallas_call | solution.py:391
  58.8 1.3 %collective-permute-done.33.rest_4_ = bf16[64,1024]{1,0:T(8,128)(2,1)S(1)} collective-permute-done((bf16[64,1024]{1,0:T(8,128)(2,1)S(1)}, bf16[64,1024]{1,0:T(8,128)(2,1)S(1)}, u32[]{:S(2)}, u32[]{:S(2)}) %collective-permute-start.33) | collective-permute-done | bytes 131104 | tf_op jit(solution)/shard_map/ppermute | solution.py:32
  60.1 0.9 %place.4 = bf16[512,1024]{1,0:T(8,128)(2,1)} custom-call(s32[17]{0:T(128)S(4)} %get-tuple-element.109.positions, bf16[64,1024]{1,0:T(8,128)(2,1)S(1)} %collective-permute-done.29.rest_0_, bf16[64,1024]{1,0:T(8,128)(2,1)S(1)} %collective-permute-done.30.rest_1_, ...), custom_call_target="tpu_custom_call", output_to_operand_aliasing={{}: (10, {})} | custom-call | tf_op jit(solution)/shard_map/place/pallas_call | solution.py:438
  61.5 3.0 %collective-permute-done.28.rest_1_ = bf16[64,1024]{1,0:T(8,128)(2,1)S(1)} collective-permute-done((bf16[64,1024]{1,0:T(8,128)(2,1)S(1)}, bf16[64,1024]{1,0:T(8,128)(2,1)S(1)}, u32[]{:S(2)}, u32[]{:S(2)}) %collective-permute-start.28) | collective-permute-done | bytes 131104 | tf_op jit(solution)/shard_map/ppermute | solution.py:32
  (41 shorter events, 7.9 us)
Async XLA Ops:
  0.8 7.0 %collective-permute-start.19 = (bf16[1,144,128]{2,1,0:T(8,128)(2,1)S(1)}, bf16[1,144,128]{2,1,0:T(8,128)(2,1)S(1)}, u32[]{:S(2)}, u32[]{:S(2)}) collective-permute-start(bf16[1,144,128]{2,1,0:T(8,128)(2,1)S(1)} %block.3.refs_0_), channel_id=1, source_target_pairs={{0,6},{1,7},{2,4},{3,5},{4,2},{5,3},{6,0},{7,1},{8,14},{9,15},{10,... | collective-permute-start | bytes 110600 | tf_op jit(solution)/shard_map/ppermute | solution.py:32
  5.9 4.9 %collective-permute-start.18 = (bf16[1,144,128]{2,1,0:T(8,128)(2,1)S(1)}, bf16[1,144,128]{2,1,0:T(8,128)(2,1)S(1)}, u32[]{:S(2)}, u32[]{:S(2)}) collective-permute-start(bf16[1,144,128]{2,1,0:T(8,128)(2,1)S(1)} %block.3.refs_0_), channel_id=1, source_target_pairs={{0,4},{1,5},{2,6},{3,7},{4,0},{5,1},{6,2},{7,3},{8,12},{9,13},{10,... | collective-permute-start | bytes 110600 | tf_op jit(solution)/shard_map/ppermute | solution.py:32
  5.9 4.9 %collective-permute-start.17 = (bf16[1,144,128]{2,1,0:T(8,128)(2,1)S(1)}, bf16[1,144,128]{2,1,0:T(8,128)(2,1)S(1)}, u32[]{:S(2)}, u32[]{:S(2)}) collective-permute-start(bf16[1,144,128]{2,1,0:T(8,128)(2,1)S(1)} %block.3.refs_0_), channel_id=1, source_target_pairs={{0,2},{1,3},{2,0},{3,1},{4,6},{5,7},{6,4},{7,5},{8,10},{9,11},{10,... | collective-permute-start | bytes 110600 | tf_op jit(solution)/shard_map/ppermute | solution.py:32
  10.7 6.4 %collective-permute-start.22 = (bf16[528,128]{1,0:T(8,128)(2,1)S(1)}, bf16[528,128]{1,0:T(8,128)(2,1)S(1)}, u32[]{:S(2)}, u32[]{:S(2)}) collective-permute-start(bf16[528,128]{1,0:T(8,128)(2,1)S(1)} %join.3.refs_0_.rest_0_), channel_id=1, source_target_pairs={{0,17},{1,16},{2,19},{3,18},{4,21},{5,20},{6,23},{7,22},{8,25},{9,... | collective-permute-start | bytes 405512 | tf_op jit(solution)/shard_map/ppermute | solution.py:32
  13.3 5.3 %collective-permute-start.21 = (bf16[528,128]{1,0:T(8,128)(2,1)S(1)}, bf16[528,128]{1,0:T(8,128)(2,1)S(1)}, u32[]{:S(2)}, u32[]{:S(2)}) collective-permute-start(bf16[528,128]{1,0:T(8,128)(2,1)S(1)} %join.3.refs_0_.rest_0_), channel_id=1, source_target_pairs={{0,16},{1,17},{2,18},{3,19},{4,20},{5,21},{6,22},{7,23},{8,24},{9,... | collective-permute-start | bytes 405512 | tf_op jit(solution)/shard_map/ppermute | solution.py:32
  13.8 5.0 %collective-permute-start.20 = (bf16[528,128]{1,0:T(8,128)(2,1)S(1)}, bf16[528,128]{1,0:T(8,128)(2,1)S(1)}, u32[]{:S(2)}, u32[]{:S(2)}) collective-permute-start(bf16[528,128]{1,0:T(8,128)(2,1)S(1)} %join.3.refs_0_.rest_0_), channel_id=1, source_target_pairs={{0,1},{1,0},{2,3},{3,2},{4,5},{5,4},{6,7},{7,6},{8,9},{9,8},{10,11... | collective-permute-start | bytes 405512 | tf_op jit(solution)/shard_map/ppermute | solution.py:32
  14.3 8.7 %collective-permute-start.25 = (bf16[528,128]{1,0:T(8,128)(2,1)S(1)}, bf16[528,128]{1,0:T(8,128)(2,1)S(1)}, u32[]{:S(2)}, u32[]{:S(2)}) collective-permute-start(bf16[528,128]{1,0:T(8,128)(2,1)S(1)} %join.3.refs_0_.rest_0_), channel_id=1, source_target_pairs={{0,8},{1,9},{2,10},{3,11},{4,12},{5,13},{6,14},{7,15},{8,0},{9,1},... | collective-permute-start | bytes 405512 | tf_op jit(solution)/shard_map/ppermute | solution.py:32
  17.1 6.7 %collective-permute-start.24 = (bf16[528,128]{1,0:T(8,128)(2,1)S(1)}, bf16[528,128]{1,0:T(8,128)(2,1)S(1)}, u32[]{:S(2)}, u32[]{:S(2)}) collective-permute-start(bf16[528,128]{1,0:T(8,128)(2,1)S(1)} %collective-permute-done.22.refs_3_.rest_0_), channel_id=1, source_target_pairs={{0,8},{1,9},{2,10},{3,11},{4,12},{5,13},{6,14},{7,15},{8,0},{9,1},... | collective-permute-start | bytes 405512 | tf_op jit(solution)/shard_map/ppermute | solution.py:32
  18.6 6.1 %collective-permute-start.23 = (bf16[528,128]{1,0:T(8,128)(2,1)S(1)}, bf16[528,128]{1,0:T(8,128)(2,1)S(1)}, u32[]{:S(2)}, u32[]{:S(2)}) collective-permute-start(bf16[528,128]{1,0:T(8,128)(2,1)S(1)} %collective-permute-done.21.refs_2_.rest_0_), channel_id=1, source_target_pairs={{0,8},{1,9},{2,10},{3,11},{4,12},{5,13},{6,14},{7,15},{8,0},{9,1},... | collective-permute-start | bytes 405512 | tf_op jit(solution)/shard_map/ppermute | solution.py:32
  18.8 7.0 %collective-permute-start.26 = (bf16[528,128]{1,0:T(8,128)(2,1)S(1)}, bf16[528,128]{1,0:T(8,128)(2,1)S(1)}, u32[]{:S(2)}, u32[]{:S(2)}) collective-permute-start(bf16[528,128]{1,0:T(8,128)(2,1)S(1)} %collective-permute-done.20.refs_1_.rest_1_), channel_id=1, source_target_pairs={{0,8},{1,9},{2,10},{3,11},{4,12},{5,13},{6,14},{7,15},{8,0},{9,1},... | collective-permute-start | bytes 405512 | tf_op jit(solution)/shard_map/ppermute | solution.py:32
  26.0 8.9 %collective-permute-start.35 = (bf16[64,1024]{1,0:T(8,128)(2,1)S(1)}, bf16[64,1024]{1,0:T(8,128)(2,1)S(1)}, u32[]{:S(2)}, u32[]{:S(2)}) collective-permute-start(bf16[64,1024]{1,0:T(8,128)(2,1)S(1)} %get-tuple-element.74.rest_0_), channel_id=1, source_target_pairs={{0,4},{1,5},{2,6},{3,7},{4,0},{5,1},{6,2},{7,3},{8,12},{9,13},{10,... | collective-permute-start | bytes 393224 | tf_op jit(solution)/shard_map/ppermute | solution.py:32
  28.1 13.2 %collective-permute-start.34 = (bf16[64,1024]{1,0:T(8,128)(2,1)S(1)}, bf16[64,1024]{1,0:T(8,128)(2,1)S(1)}, u32[]{:S(2)}, u32[]{:S(2)}) collective-permute-start(bf16[64,1024]{1,0:T(8,128)(2,1)S(1)} %get-tuple-element.74.rest_0_), channel_id=1, source_target_pairs={{0,2},{1,3},{2,0},{3,1},{4,6},{5,7},{6,4},{7,5},{8,10},{9,11},{10,... | collective-permute-start | bytes 393224 | tf_op jit(solution)/shard_map/ppermute | solution.py:32
  34.9 8.1 %collective-permute-start.36 = (bf16[64,1024]{1,0:T(8,128)(2,1)S(1)}, bf16[64,1024]{1,0:T(8,128)(2,1)S(1)}, u32[]{:S(2)}, u32[]{:S(2)}) collective-permute-start(bf16[64,1024]{1,0:T(8,128)(2,1)S(1)} %collective-permute-done.35.rest_2_.rest_6_), channel_id=1, source_target_pairs={{0,2},{1,3},{2,0},{3,1},{4,6},{5,7},{6,4},{7,5},{8,10},{9,11},{10,... | collective-permute-start | bytes 393224 | tf_op jit(solution)/shard_map/ppermute | solution.py:32
  35.5 10.2 %collective-permute-start.29 = (bf16[64,1024]{1,0:T(8,128)(2,1)S(1)}, bf16[64,1024]{1,0:T(8,128)(2,1)S(1)}, u32[]{:S(2)}, u32[]{:S(2)}) collective-permute-start(bf16[64,1024]{1,0:T(8,128)(2,1)S(1)} %get-tuple-element.69), channel_id=1, source_target_pairs={{0,7},{1,6},{2,5},{3,4},{4,3},{5,2},{6,1},{7,0},{8,15},{9,14},{10,... | collective-permute-start | bytes 393224 | tf_op jit(solution)/shard_map/ppermute | solution.py:32
  39.2 9.6 %collective-permute-start.30 = (bf16[64,1024]{1,0:T(8,128)(2,1)S(1)}, bf16[64,1024]{1,0:T(8,128)(2,1)S(1)}, u32[]{:S(2)}, u32[]{:S(2)}) collective-permute-start(bf16[64,1024]{1,0:T(8,128)(2,1)S(1)} %get-tuple-element.70), channel_id=1, source_target_pairs={{0,1},{1,0},{2,3},{3,2},{4,5},{5,4},{6,7},{7,6},{8,9},{9,8},{10,11... | collective-permute-start | bytes 393224 | tf_op jit(solution)/shard_map/ppermute | solution.py:32
  39.8 16.3 %collective-permute-start.31 = (bf16[64,1024]{1,0:T(8,128)(2,1)S(1)}, bf16[64,1024]{1,0:T(8,128)(2,1)S(1)}, u32[]{:S(2)}, u32[]{:S(2)}) collective-permute-start(bf16[64,1024]{1,0:T(8,128)(2,1)S(1)} %get-tuple-element.71), channel_id=1, source_target_pairs={{0,6},{1,7},{2,4},{3,5},{4,2},{5,3},{6,0},{7,1},{8,14},{9,15},{10,... | collective-permute-start | bytes 393224 | tf_op jit(solution)/shard_map/ppermute | solution.py:32
  41.3 17.4 %collective-permute-start.32 = (bf16[64,1024]{1,0:T(8,128)(2,1)S(1)}, bf16[64,1024]{1,0:T(8,128)(2,1)S(1)}, u32[]{:S(2)}, u32[]{:S(2)}) collective-permute-start(bf16[64,1024]{1,0:T(8,128)(2,1)S(1)} %get-tuple-element.72), channel_id=1, source_target_pairs={{0,3},{1,2},{2,1},{3,0},{4,7},{5,6},{6,5},{7,4},{8,11},{9,10},{10,... | collective-permute-start | bytes 393224 | tf_op jit(solution)/shard_map/ppermute | solution.py:32
  43.1 17.0 %collective-permute-start.33 = (bf16[64,1024]{1,0:T(8,128)(2,1)S(1)}, bf16[64,1024]{1,0:T(8,128)(2,1)S(1)}, u32[]{:S(2)}, u32[]{:S(2)}) collective-permute-start(bf16[64,1024]{1,0:T(8,128)(2,1)S(1)} %get-tuple-element.73), channel_id=1, source_target_pairs={{0,5},{1,4},{2,7},{3,6},{4,1},{5,0},{6,3},{7,2},{8,13},{9,12},{10,... | collective-permute-start | bytes 393224 | tf_op jit(solution)/shard_map/ppermute | solution.py:32
  45.7 14.3 %collective-permute-start.37 = (bf16[64,1024]{1,0:T(8,128)(2,1)S(1)}, bf16[64,1024]{1,0:T(8,128)(2,1)S(1)}, u32[]{:S(2)}, u32[]{:S(2)}) collective-permute-start(bf16[64,1024]{1,0:T(8,128)(2,1)S(1)} %choose.1), channel_id=1, source_target_pairs={{0,1},{1,0},{2,3},{3,2},{4,5},{5,4},{6,7},{7,6},{8,9},{9,8},{10,11... | collective-permute-start | bytes 393224 | tf_op jit(solution)/shard_map/ppermute | solution.py:32
  48.9 12.7 %collective-permute-start.27 = (bf16[64,1024]{1,0:T(8,128)(2,1)S(1)}, bf16[64,1024]{1,0:T(8,128)(2,1)S(1)}, u32[]{:S(2)}, u32[]{:S(2)}) collective-permute-start(bf16[64,1024]{1,0:T(8,128)(2,1)S(1)} %get-tuple-element.67), channel_id=1, source_target_pairs={{0,2},{1,3},{2,0},{3,1},{4,6},{5,7},{6,4},{7,5},{8,10},{9,11},{10,... | collective-permute-start | bytes 393224 | tf_op jit(solution)/shard_map/ppermute | solution.py:32
  56.1 8.5 %copy-start = (bf16[1,128,128]{2,1,0:T(8,128)(2,1)S(1)}, bf16[1,128,128]{2,1,0:T(8,128)(2,1)}, u32[]{:S(2)}) copy-start(bf16[1,128,128]{2,1,0:T(8,128)(2,1)} %integrals.1) | copy-start | bytes 98308
  56.1 8.5 %copy-start.1 = (s32[8,32]{1,0:T(8,128)S(1)}, s32[8,32]{1,0:T(8,128)}, u32[]{:S(2)}) copy-start(s32[8,32]{1,0:T(8,128)} %live.1) | copy-start | bytes 3076
  56.1 8.5 %copy-start.2 = (s32[8]{0:T(128)S(1)}, s32[8]{0:T(128)}, u32[]{:S(2)}) copy-start(s32[8]{0:T(128)} %destination.1) | copy-start | bytes 100
  56.1 8.5 %collective-permute-start.28 = (bf16[64,1024]{1,0:T(8,128)(2,1)S(1)}, bf16[64,1024]{1,0:T(8,128)(2,1)S(1)}, u32[]{:S(2)}, u32[]{:S(2)}) collective-permute-start(bf16[64,1024]{1,0:T(8,128)(2,1)S(1)} %get-tuple-element.68), channel_id=1, source_target_pairs={{0,4},{1,5},{2,6},{3,7},{4,0},{5,1},{6,2},{7,3},{8,12},{9,13},{10,... | collective-permute-start | bytes 393224 | tf_op jit(solution)/shard_map/ppermute | solution.py:32
  (1 other events, 8.5 us)
